TPU v7x, 32 devices: a whole 2x2x4 slice. The times are simulated.
32 devices in a mesh: group: 2 (over x), date: 16 (over z, y, core).
Axes of the slice: x: 2, y: 2, z: 4, core: 2. Of those that a mesh axis runs over, the one named last changes fastest.
Arguments:
- slc_stack: bfloat16 [16, 2, 32, 16384], P('date', None, 'group'), parts along dimension 2, may hold values from -30 to 30
- band_taps: bfloat16 [2, 2, 32], replicated, may hold values from -1 to 1
- pair_flags: int32 [16, 4], P('date'), may hold values from 0 to 1, as said below
Outputs:
- iono_phase: float32 [16, 8, 1024], P('date', 'group'), parts along dimension 1
- weight_sum: float32 [16, 8, 1024], P('date', 'group'), parts along dimension 1
There are 2 independent parts, one for each index of `group`. A program takes and returns all parts, laid end to end along the dimension named above; an argument that names none is the same for every part. Nothing has to cross between parts.
Inputs may be any that keep to these rules, and one draw needn't show every extreme that they name: pair_flags[d,0] is 1 for every date but the last; pair_flags[d,k] is 0 where d + k + 1 >= 16.
All inputs are finite; a program needn't handle non-finite values.
Results may differ from a plain program's by a relative error of at most 0.002.
Values may be sent and summed in bfloat16 or wider, within the bound.
A program may use at most 128 MiB of HBM per device.

v0:
```python
import functools

import jax
import jax.numpy as jnp
from jax import lax
from jax.experimental import pallas as pl
from jax.experimental.pallas import tpu as pltpu
from jax.sharding import PartitionSpec as P

TAPS = 32
ML_AZ = 4
ML_RG = 16
SPAN = 4
RADIUS = 8
ITERS = 4

LANES = 128
CELLS = LANES // ML_RG

eps_power = 1e-06
floor_weight = 0.1
ridge_weight = 0.05
split_coef = 2.0

F32 = jnp.float32
BF16 = jnp.bfloat16


def kernel(
    n, n_rg, pieces, cuts,
    slc_hbm, flags_hbm, taps_hbm, out_ref,
    slc, flags_in, taps_in, taps_ref, data, own_flags, recv, flags, mat, filt, bands, power, cross, wgt, phs, phi_a, phi_b,
    rhs, inv, wsum, pack, back,
    in_sem, send_sem, recv_sem, fsend_sem, frecv_sem, osend_sem, orecv_sem,
):
    me = lax.axis_index("date")
    blocks = pieces - 1
    own_blocks = pieces - 4
    rows_pad = bands.shape[2]
    my_q = lax.rem(me, n_rg)

    slc_load = pltpu.make_async_copy(slc_hbm.at[0], slc, in_sem.at[0])
    slc_load.start()
    flags_load = pltpu.make_async_copy(flags_hbm, flags_in, in_sem.at[1])
    flags_load.start()
    taps_load = pltpu.make_async_copy(taps_hbm, taps_in, in_sem.at[2])
    taps_load.start()
    barrier = pltpu.get_barrier_semaphore()

    def greet(i, carry):
        other = lax.rem(me + i, n)
        pl.semaphore_signal(
            barrier, inc=1, device_id={"date": other}, device_id_type=pl.DeviceIdType.MESH
        )
        return carry

    lax.fori_loop(1, n, greet, 0)

    flags_load.wait()
    own_flags[...] = jnp.zeros_like(own_flags)
    own_flags[0:1, 0:SPAN] = flags_in[...].astype(F32)
    taps_load.wait()
    taps_ref[...] = jnp.zeros_like(taps_ref)
    for band in range(2):
        taps_ref[2 * band:2 * band + 2, 0:TAPS] = taps_in[band].astype(F32)
    slc_load.wait()

    n_az = n // n_rg
    n_tiles = data.shape[1] // 16
    n_blocks = slc.shape[2] // LANES
    upper = lax.broadcasted_iota(jnp.int32, (8, LANES), 0) < ML_AZ

    def regroup(tile, lo, hi):
        for part in range(2):
            for half in range(n_az // 2):
                made = ([], [])
                for pair in range(2):
                    two = []
                    for m in (2 * pair, 2 * pair + 1):
                        if lo <= m < hi:
                            at = pl.multiple_of((4 * tile - 2 + m) * LANES, LANES)
                            value = slc[part, :, pl.ds(at, LANES)].astype(F32)
                            two.append(value[8 * half:8 * half + 8])
                        else:
                            two.append(jnp.zeros((8, LANES), F32))
                    made[0].append(jnp.where(upper, two[0], pltpu.roll(two[1], ML_AZ, 0)))
                    made[1].append(jnp.where(upper, pltpu.roll(two[0], ML_AZ, 0), two[1]))
                for odd in range(2):
                    value = jnp.concatenate(made[odd], axis=0).astype(BF16)
                    to = pl.multiple_of(tile * 16, 16)
                    data[2 * half + odd, pl.ds(to, 16), part * LANES:part * LANES + LANES] = value

    def inner_tile(tile, carry):
        regroup(tile, 0, 4)
        return carry

    lax.fori_loop(1, n_tiles - 1, inner_tile, 0, unroll=False)
    regroup(0, 2, 4)
    regroup(n_tiles - 1, 0, 2)

    chunk_rows = ML_AZ * pieces
    stride_rows = ML_AZ * own_blocks

    def strip_of(ref, strip):
        lo, hi = cuts[strip], cuts[strip + 1]
        return ref.at[pl.ds(lo, hi - lo)]

    def source(target, strip):
        lo, hi = cuts[strip], cuts[strip + 1]
        begin = pl.multiple_of(lax.rem(target, n_rg) * stride_rows + lo, 16)
        return data.at[target // n_rg, pl.ds(begin, hi - lo)]

    def data_copy(target, strip):
        return pltpu.make_async_remote_copy(
            src_ref=source(target, strip), dst_ref=strip_of(recv.at[me], strip),
            send_sem=send_sem.at[strip, target], recv_sem=recv_sem.at[strip, me],
            device_id={"date": target}, device_id_type=pl.DeviceIdType.MESH,
        )

    def flag_copy(target):
        return pltpu.make_async_remote_copy(
            src_ref=own_flags, dst_ref=flags.at[me + SPAN],
            send_sem=fsend_sem.at[target], recv_sem=frecv_sem.at[me],
            device_id={"date": target}, device_id_type=pl.DeviceIdType.MESH,
        )

    for strip in range(2):
        pltpu.make_async_copy(
            source(me, strip), strip_of(recv.at[me], strip), recv_sem.at[strip, me]
        ).start()
    pltpu.make_async_copy(own_flags, flags.at[me + SPAN], frecv_sem.at[me]).start()

    pl.semaphore_wait(barrier, n - 1)

    def send_strip(strip):
        def send_pair(i, carry):
            for target, go in ((n - 1 - i, n - 1 - i > me), (i, i < me)):
                @pl.when(go)
                def _():
                    data_copy(target, strip).start()
                    if strip == 0:
                        flag_copy(target).start()
            return carry

        lax.fori_loop(0, n, send_pair, 0)

    send_strip(0)
    send_strip(1)

    k_id = lax.broadcasted_iota(jnp.int32, (LANES, LANES), 0)
    j_id = lax.broadcasted_iota(jnp.int32, (LANES, LANES), 1)
    circ = []
    for m in range(4):
        base = jnp.broadcast_to(taps_ref[m:m + 1, :], (LANES, LANES))
        circ.append(pltpu.roll(base, 0, 1, stride=1, stride_axis=0).T)
    for half in range(2):
        keep = (j_id <= k_id) if half == 0 else (j_id > k_id)
        for band in range(2):
            re_part = jnp.where(keep, circ[2 * band], 0.0).astype(BF16)
            im_value = jnp.where(keep, circ[2 * band + 1], 0.0)
            im_part = im_value.astype(BF16)
            im_minus = (-im_value).astype(BF16)
            col = half * 512 + band * 256
            mat[0:128, col:col + 128] = re_part
            mat[0:128, col + 128:col + 256] = im_part
            mat[128:256, col:col + 128] = im_minus
            mat[128:256, col + 128:col + 256] = re_part

    for ref in (bands, power, cross, wgt, phs, phi_a, phi_b):
        ref[...] = jnp.zeros_like(ref)
    flags[0:SPAN] = jnp.zeros((SPAN,) + flags.shape[1:], F32)

    cell_row = lax.broadcasted_iota(jnp.int32, (CELLS, 4 * LANES), 0)
    lane = lax.broadcasted_iota(jnp.int32, (CELLS, 4 * LANES), 1)
    pick = lax.rem(lane, LANES) // ML_RG == cell_row
    sum_re = jnp.where(pick, 1.0, 0.0).astype(BF16)
    sum_im = jnp.where(pick, jnp.where(lax.rem(lane, 2 * LANES) < LANES, -1.0, 1.0), 0.0).astype(BF16)
    contract = (((1,), (1,)), ((), ()))

    def looks(value, selector):
        high = value.astype(BF16)
        low = (value - high.astype(F32)).astype(BF16)
        both = jnp.concatenate([high, low], axis=1)
        return lax.dot_general(selector, both, contract, preferred_element_type=F32)

    ring = bands.shape[0]

    group = 4 if n % 4 == 0 else 1

    def some_dates(strip, i):
        r0, r1 = cuts[strip], cuts[strip + 1]
        first = max(r0 - ML_AZ, 0)
        b0 = first // ML_AZ
        count = (r1 - first) // ML_AZ - 1
        pad = -(-count // 8) * 8
        base = first // 16 * 16
        off = first - base
        high_rows = r1 - base
        for u in range(group):
            d = i * group + u
            pltpu.make_async_copy(
                strip_of(recv.at[d], strip), strip_of(recv.at[d], strip), recv_sem.at[strip, d]
            ).wait()
            if strip == 0:
                pltpu.make_async_copy(
                    flags.at[d + SPAN], flags.at[d + SPAN], frecv_sem.at[d]
                ).wait()
        pieces_in = [recv[i * group + u, base:r1] for u in range(group)]
        made = jnp.dot(
            jnp.concatenate(pieces_in, axis=0), mat[...], preferred_element_type=F32
        )
        for g in range(8):
            filt[g, 0:group * high_rows, :] = made[:, g * LANES:g * LANES + LANES]
        for u in range(group):
            slot = lax.rem(i * group + u, ring)
            for r in range(ML_AZ):
                for g in range(4):
                    start = u * high_rows + off + r
                    low = filt[g, pl.ds(start, count, stride=ML_AZ), :]
                    high = filt[g + 4, pl.ds(start + ML_AZ, count, stride=ML_AZ), :]
                    value = (low + high).astype(BF16).astype(F32)
                    bands[slot, r, 0:count, g * LANES:g * LANES + LANES] = value
        for u in range(group):
            d = i * group + u
            slot = lax.rem(d, ring)
            re_list = []
            im_list = []
            for band in range(2):
                cols = slice(band * 256, band * 256 + 256)
                for k in range(SPAN + 1):
                    early = lax.rem(d + ring - k, ring)
                    total_re = None
                    total_im = None
                    for r in range(ML_AZ):
                        a = bands[early, r, 0:pad, cols]
                        b = bands[slot, r, 0:pad, cols]
                        total_re = a * b if r == 0 else total_re + a * b
                        if k > 0:
                            b_swap = jnp.concatenate([b[:, 128:], b[:, :128]], axis=1)
                            total_im = a * b_swap if r == 0 else total_im + a * b_swap
                    re_list.append(total_re)
                    if k > 0:
                        im_list.append(total_im)
            re_looks = looks(jnp.concatenate(re_list, axis=0), sum_re)
            im_looks = looks(jnp.concatenate(im_list, axis=0), sum_im)
            for band in range(2):
                at = band * (SPAN + 1) * pad
                power[band, d + SPAN, :, b0:b0 + count] = re_looks[:, at:at + count]
                for k in range(1, SPAN + 1):
                    at = (band * (SPAN + 1) + k) * pad
                    cross[k - 1, 2 * band, d - k + SPAN, :, b0:b0 + count] = re_looks[:, at:at + count]
                    at = (band * SPAN + k - 1) * pad
                    cross[k - 1, 2 * band + 1, d - k + SPAN, :, b0:b0 + count] = im_looks[:, at:at + count]

    for strip in range(2):

        def step_dates(i, carry):
            some_dates(strip, i)
            return carry

        lax.fori_loop(0, n // group, step_dates, 0)

    step = min(8, n)
    shape = (step, CELLS, LANES)
    c_id = lax.broadcasted_iota(jnp.int32, shape, 1)
    b_id = lax.broadcasted_iota(jnp.int32, shape, 2)
    cell = CELLS * (own_blocks * my_q - 2 + b_id) + 1 + c_id
    valid = (b_id < blocks) & (cell >= 0) & (cell < n_rg * own_blocks * CELLS)

    def box(value):
        value = jnp.where(valid, value, 0.0)
        prefix = value
        for hop in (1, 2, 4):
            prefix = prefix + jnp.where(c_id >= hop, pltpu.roll(prefix, hop, 1), 0.0)
        whole = jnp.sum(value, axis=1, keepdims=True)
        suffix = whole - prefix + value
        return pltpu.roll(suffix, 1, 2) + whole + pltpu.roll(prefix, LANES - 1, 2)

    f_lane = lax.broadcasted_iota(jnp.int32, (step, 1, LANES), 2)

    def smooth(i, carry):
        at = i * step + SPAN
        for k in range(SPAN):
            cr0, ci0, cr1, ci1 = (cross[k, m, pl.ds(at, step)] for m in range(4))
            ab0 = power[0, pl.ds(at, step)] * power[0, pl.ds(at + k + 1, step)] + eps_power
            ab1 = power[1, pl.ds(at, step)] * power[1, pl.ds(at + k + 1, step)] + eps_power
            flag = jnp.sum(jnp.where(f_lane == k, flags[pl.ds(at, step)], 0.0), axis=2, keepdims=True)
            weight = flag * 0.5 * ((cr0 * cr0 + ci0 * ci0) / ab0 + (cr1 * cr1 + ci1 * ci1) / ab1)
            phase = split_coef * (ci0 * cr1 - cr0 * ci1) / jnp.sqrt(ab0 * ab1)
            den = box(weight)
            num = box(weight * phase)
            phs[k, pl.ds(at, step)] = num / (den + floor_weight)
            wgt[k, pl.ds(at, step)] = den / (2 * RADIUS + 1)
        return carry

    lax.fori_loop(0, n // step, smooth, 0)

    def chain(d, state):
        phi_a[d + SPAN] = state
        return state + phs[0, d + SPAN]

    lax.fori_loop(0, n, chain, jnp.zeros((CELLS, LANES), F32))

    def constants(i, carry):
        at = i * step + SPAN
        total = jnp.zeros(shape, F32)
        acc = ridge_weight * phi_a[pl.ds(at, step)]
        for k in range(1, SPAN + 1):
            w = wgt[k - 1, pl.ds(at, step)]
            low = wgt[k - 1, pl.ds(at - k, step)]
            total = total + w + low
            acc = acc - w * phs[k - 1, pl.ds(at, step)] + low * phs[k - 1, pl.ds(at - k, step)]
        wsum[pl.ds(i * step, step)] = total
        rhs[pl.ds(i * step, step)] = acc
        inv[pl.ds(i * step, step)] = 1.0 / (total + ridge_weight)
        return carry

    lax.fori_loop(0, n // step, constants, 0)

    for sweep in range(ITERS):
        old, new = (phi_a, phi_b) if sweep % 2 == 0 else (phi_b, phi_a)

        def relax(i, carry):
            at = i * step + SPAN
            acc = rhs[pl.ds(i * step, step)]
            for k in range(1, SPAN + 1):
                acc = acc + wgt[k - 1, pl.ds(at, step)] * old[pl.ds(at + k, step)]
                acc = acc + wgt[k - 1, pl.ds(at - k, step)] * old[pl.ds(at - k, step)]
            new[pl.ds(at, step)] = acc * inv[pl.ds(i * step, step)]
            return carry

        lax.fori_loop(0, n // step, relax, 0)
    last = phi_a if ITERS % 2 == 0 else phi_b

    def align(value):
        down = pltpu.roll(value, 1, 1)
        return jnp.where(c_id == 0, pltpu.roll(down, LANES - 1, 2), pltpu.roll(down, LANES - 2, 2))

    def finish(i, carry):
        phase = align(last[pl.ds(i * step + SPAN, step)])
        total = align(wsum[pl.ds(i * step, step)])
        pack[pl.ds(i * step, step)] = jnp.where(b_id < 64, phase, pltpu.roll(total, 64, 2))
        return carry

    lax.fori_loop(0, n // step, finish, 0)

    def out_copy(target):
        return pltpu.make_async_remote_copy(
            src_ref=pack.at[target], dst_ref=back.at[me],
            send_sem=osend_sem.at[target], recv_sem=orecv_sem.at[me],
            device_id={"date": target}, device_id_type=pl.DeviceIdType.MESH,
        )

    own_back = pltpu.make_async_copy(pack.at[me], back.at[me], orecv_sem.at[me])
    own_back.start()

    def send_back(i, carry):
        out_copy(lax.rem(me + i, n)).start()
        return carry

    lax.fori_loop(1, n, send_back, 0)

    def drain(i, carry):
        target = lax.rem(me + i, n)
        data_copy(target, 0).wait_send()
        data_copy(target, 1).wait_send()
        flag_copy(target).wait_send()
        out_copy(target).wait_send()
        return carry

    lax.fori_loop(1, n, drain, 0)

    def arrive(s, carry):
        pltpu.make_async_copy(back.at[s], back.at[s], orecv_sem.at[s]).wait()
        return carry

    lax.fori_loop(0, n, arrive, 0)

    wide = own_blocks * CELLS
    value = back[...].reshape(n * CELLS, LANES)
    high = value.astype(BF16)
    rest = value - high.astype(F32)
    middle = rest.astype(BF16)
    low = (rest - middle.astype(F32)).astype(BF16)
    place_row = lax.broadcasted_iota(jnp.int32, (LANES, 2 * wide), 0)
    place_col = lax.broadcasted_iota(jnp.int32, (LANES, 2 * wide), 1)
    place_row_of = (place_col // wide) * 64 + lax.rem(place_col, wide) // CELLS
    place = jnp.where(place_row == place_row_of, 1.0, 0.0).astype(BF16)
    spread = jnp.dot(
        jnp.concatenate([high, middle, low], axis=0), place, preferred_element_type=F32
    )
    count = n * CELLS
    spread = spread[0:count] + spread[count:2 * count] + spread[2 * count:3 * count]
    spread = spread.reshape(n, CELLS, 2 * wide)
    s_row = lax.broadcasted_iota(jnp.int32, spread.shape, 1)
    s_col = lax.broadcasted_iota(jnp.int32, spread.shape, 2)
    rows = jnp.sum(jnp.where(lax.rem(s_col, CELLS) == s_row, spread, 0.0), axis=1)
    for s in range(n):
        az, q = s // n_rg, s % n_rg
        out_ref[0, az:az + 1, q * wide:q * wide + wide] = rows[s:s + 1, 0:wide]
        out_ref[1, az:az + 1, q * wide:q * wide + wide] = rows[s:s + 1, wide:2 * wide]


def local(slc_stack, band_taps, pair_flags):
    n = lax.axis_size("date")
    rows, span = slc_stack.shape[2:]
    n_az = rows // ML_AZ
    n_rg = n // n_az
    own_blocks = span // LANES // n_rg
    pieces = own_blocks + 4
    rows_pad = -(-(pieces - 1) // 8) * 8
    chunk_rows = ML_AZ * pieces

    half = -(-chunk_rows // 32) * 16
    cuts = (0, half, chunk_rows)
    padded_rows = ML_AZ * (span // LANES + 4)

    vmem = pl.BlockSpec(memory_space=pltpu.VMEM)
    small = lambda *lead: pltpu.VMEM((*lead, CELLS, LANES), F32)
    ring = 2 * SPAN
    sem = pltpu.SemaphoreType.DMA((n,))
    two_sem = pltpu.SemaphoreType.DMA((2, n))
    both = pl.pallas_call(
        functools.partial(kernel, n, n_rg, pieces, cuts),
        out_shape=jax.ShapeDtypeStruct((2, n_az, span // ML_RG), F32),
        in_specs=[pl.BlockSpec(memory_space=pl.ANY)] * 3,
        out_specs=vmem,
        scratch_shapes=[
            pltpu.VMEM((2, rows, span), BF16),
            pltpu.VMEM((1, SPAN), jnp.int32),
            pltpu.VMEM((2, 2, TAPS), BF16),
            pltpu.VMEM((8, LANES), F32),
            pltpu.VMEM((n_az, padded_rows, 2 * LANES), BF16),
            pltpu.VMEM((1, LANES), F32),
            pltpu.VMEM((n, chunk_rows, 2 * LANES), BF16),
            pltpu.VMEM((n + SPAN, 1, LANES), F32),
            pltpu.VMEM((256, 1024), BF16),
            pltpu.VMEM((8, 4 * chunk_rows, LANES), F32),
            pltpu.VMEM((ring, ML_AZ, rows_pad, 512), F32),
            small(2, n + 2 * SPAN),
            small(SPAN, 4, n + 2 * SPAN),
            small(SPAN, n + 2 * SPAN),
            small(SPAN, n + 2 * SPAN),
            small(n + 2 * SPAN),
            small(n + 2 * SPAN),
            small(n),
            small(n),
            small(n),
            small(n),
            small(n),
            pltpu.SemaphoreType.DMA((3,)), two_sem, two_sem, sem, sem, sem, sem,
        ],
        compiler_params=pltpu.CompilerParams(
            collective_id=0, has_side_effects=True, vmem_limit_bytes=60 * 1024 * 1024
        ),
    )(slc_stack, pair_flags, band_taps)
    return both[0:1], both[1:2]


def solution(mesh):
    in_specs = (P("date", None, "group", None), P(), P("date", None))
    out_specs = (P("date", "group", None), P("date", "group", None))
    return jax.shard_map(local, mesh=mesh, in_specs=in_specs, out_specs=out_specs, check_vma=False)
```

profile of v0, /device:TPU:0, one launch (start us, length us, event | category | flops | bytes accessed | tf_op | source)
XLA Modules:
  0.0 45.6 jit_solution(13474587668521934551)
XLA Ops:
  0.6 43.6 %shard_map.50 = f32[2,4,1024]{2,1,0:T(4,128)} custom-call(bf16[1,2,16,16384]{3,2,1,0:T(8,128)(2,1)} %slc_hbm.1, s32[1,4]{1,0:T(1,128)} %flags_hbm.1, bf16[2,2,32]{2,1,0:T(2,128)(2,1)} %taps_hbm.1), custom_call_target="tpu_custom_call" | custom-call | tf_op jit(solution)/shard_map/pallas_call | solution.py:423
  44.2 1.3 %fusion = (f32[1,4,1024]{2,1,0:T(4,128)}, f32[1,4,1024]{2,1,0:T(4,128)}) fusion(f32[2,4,1024]{2,1,0:T(4,128)} %shard_map.50), kind=kLoop, calls=%fused_computation | loop fusion | bytes 65536 | tf_op jit(solution)/shard_map/slice | solution.py:457
where the time goes:
time: 45.8 us; the launch traced here: 45.6 us
  Pallas kernels  43.6 us (95%)
  local copies, waits for them, and re-layouts  1.35 us (3%)
  between operations  0.64 us (1%)
    pallas_call x1, Pallas kernels, local(): pl.pallas_call(functools.partial(kernel, n, n_rg, pieces, cuts), out_shap...  43.6 us
    slice x1, local copies, waits for them, and re-layouts, local(): return (both[0:1], both[1:2])  1.35 us

commit v1 on v0

v1 whole, which is shorter than its diff:
```python
import functools

import jax
import jax.numpy as jnp
from jax import lax
from jax.experimental import pallas as pl
from jax.experimental.pallas import tpu as pltpu
from jax.sharding import PartitionSpec as P

TAPS = 32
ML_AZ = 4
ML_RG = 16
SPAN = 4
RADIUS = 8
ITERS = 4

LANES = 128
CELLS = LANES // ML_RG
SUB = 16
SIDE = SPAN // 2
WIN = SPAN + 2 * SIDE
SLOT = ML_AZ + 1

eps_power = 1e-06
floor_weight = 0.1
ridge_weight = 0.05
split_coef = 2.0

F32 = jnp.float32
BF16 = jnp.bfloat16

OWN = tuple(range(SIDE, SIDE + SPAN))
FAR = tuple(range(SIDE)) + tuple(range(SIDE + SPAN, WIN))


def first_date(k):
    return 0 if k == SPAN else 1


PAIRS = [(first_date(k) + g, k) for k in range(1, SPAN + 1) for g in range(SPAN)]
OWN_PAIRS = [(w, k) for w, k in PAIRS if w in OWN and w + k in OWN]
FAR_PAIRS = [p for p in PAIRS if p not in OWN_PAIRS]


def listing():
    order = {}
    for dates, pairs in ((OWN, OWN_PAIRS), (FAR, FAR_PAIRS)):
        for w in dates:
            for band in range(2):
                order["p", w, band] = len(order)
        for w, k in pairs:
            for band in range(2):
                order["r", w, k, band] = len(order)
                order["i", w, k, band] = len(order)
    return order


ORDER = listing()
OWN_COUNT = 2 * SPAN + 4 * len(OWN_PAIRS)
FAR_COUNT = 2 * SPAN + 4 * len(FAR_PAIRS)


def kernel(
    n, steps,
    slc_hbm, flags_hbm, taps_hbm, out_ref,
    slc, flags_in, taps_in, taps_ref, turn, data, recv, mat, bands_own, bands_far, both, red, qty, quant,
    msg, got, fin, pack, back,
    in_sem, send_sem, recv_sem, fsend_sem, bsend_sem, brecv_sem, dsend_sem, drecv_sem, wave_sem,
):
    me = lax.axis_index("date")
    q = lax.rem(me, SPAN)
    z = me // SPAN
    slabs = n // SPAN
    wide = LANES // slabs
    has_left = z > 0
    has_right = z < slabs - 1
    mesh_id = pl.DeviceIdType.MESH

    slc_load = pltpu.make_async_copy(slc_hbm.at[0], slc, in_sem.at[0])
    slc_load.start()
    flags_load = pltpu.make_async_copy(flags_hbm, flags_in, in_sem.at[1])
    flags_load.start()
    taps_load = pltpu.make_async_copy(taps_hbm, taps_in, in_sem.at[2])
    taps_load.start()
    barrier = pltpu.get_barrier_semaphore()

    for hop in range(1, SPAN):
        pl.semaphore_signal(
            barrier, inc=1, device_id={"date": z * SPAN + lax.rem(q + hop, SPAN)}, device_id_type=mesh_id
        )

    @pl.when(has_left)
    def _():
        pl.semaphore_signal(barrier, inc=1, device_id={"date": me - SPAN}, device_id_type=mesh_id)

    @pl.when(has_right)
    def _():
        pl.semaphore_signal(barrier, inc=1, device_id={"date": me + SPAN}, device_id_type=mesh_id)

    flags_load.wait()
    tile_row = lax.broadcasted_iota(jnp.int32, (SUB, 2 * LANES), 0)
    own_flags = flags_in[...].astype(F32)
    flag_tile = jnp.zeros((SUB, 2 * LANES), F32)
    for k in range(SPAN):
        flag_tile = jnp.where(tile_row == k, jnp.broadcast_to(own_flags[0:1, k:k + 1], flag_tile.shape), flag_tile)
    flag_tile = flag_tile.astype(BF16)
    for s in range(SPAN):
        data[s, SLOT + ML_AZ] = flag_tile
    taps_load.wait()
    taps_ref[...] = jnp.zeros_like(taps_ref)
    for band in range(2):
        taps_ref[2 * band:2 * band + 2, 0:TAPS] = taps_in[band].astype(F32)

    k_id = lax.broadcasted_iota(jnp.int32, (LANES, LANES), 0)
    j_id = lax.broadcasted_iota(jnp.int32, (LANES, LANES), 1)
    reach = k_id - j_id + TAPS // 2
    circ = []
    for m in range(4):
        base = jnp.broadcast_to(taps_ref[m:m + 1, :], (LANES, LANES))
        circ.append(pltpu.roll(base, LANES - TAPS // 2, 1, stride=1, stride_axis=0).T)
    for edge in range(2):
        inside = (reach >= 0) & (reach < LANES)
        keep = inside if edge == 0 else jnp.logical_not(inside)
        row = edge * 2 * LANES
        for band in range(2):
            re_part = jnp.where(keep, circ[2 * band], 0.0).astype(BF16)
            im_value = jnp.where(keep, circ[2 * band + 1], 0.0)
            im_part = im_value.astype(BF16)
            im_minus = (-im_value).astype(BF16)
            col = band * 2 * LANES
            mat[row:row + 128, col:col + 128] = re_part
            mat[row:row + 128, col + 128:col + 256] = im_part
            mat[row + 128:row + 256, col:col + 128] = im_minus
            mat[row + 128:row + 256, col + 128:col + 256] = re_part

    slc_load.wait()

    def regroup(j, carry):
        for part in range(2):
            for i in range(SUB):
                at = pl.multiple_of((steps * i + j) * LANES, LANES)
                value = slc[part, :, pl.ds(at, LANES)].astype(F32)
                turn[pl.ds(part * SUB * SUB + i, SUB, stride=SUB), :] = value
        for part in range(2):
            for s in range(SPAN):
                for r in range(ML_AZ):
                    row = part * SUB * SUB + (ML_AZ * s + r) * SUB
                    value = turn[row:row + SUB, :].astype(BF16)
                    data[s, SLOT * (j + 1) + r, :, part * LANES:part * LANES + LANES] = value
        return carry

    lax.fori_loop(0, steps, regroup, 0)

    def chunk(ref, j, first):
        return ref.at[pl.ds(SLOT * (j + 1), SLOT if first else ML_AZ)]

    def slab_copy(target, j, first):
        return pltpu.make_async_remote_copy(
            src_ref=chunk(data.at[target], j, first), dst_ref=chunk(recv.at[q + SIDE], j, first),
            send_sem=send_sem.at[target, j], recv_sem=recv_sem.at[q + SIDE, j],
            device_id={"date": z * SPAN + target}, device_id_type=mesh_id,
        )

    def own_copy(j, first):
        return pltpu.make_async_copy(
            chunk(data.at[q], j, first), chunk(recv.at[q + SIDE], j, first), recv_sem.at[q + SIDE, j]
        )

    def side_copy(w, j, first):
        go_left = w < SPAN
        to, device = (w + SPAN, me - SPAN) if go_left else (w - SPAN, me + SPAN)
        return pltpu.make_async_remote_copy(
            src_ref=chunk(recv.at[w], j, first), dst_ref=chunk(recv.at[to], j, first),
            send_sem=fsend_sem.at[w - SIDE, j], recv_sem=recv_sem.at[to, j],
            device_id={"date": device}, device_id_type=mesh_id,
        )

    def arrived(w, j, first):
        ref = chunk(recv.at[w], j, first)
        pltpu.make_async_copy(ref, ref, recv_sem.at[w, j]).wait()

    near = SPAN - 1 + has_left.astype(jnp.int32) + has_right.astype(jnp.int32)
    pl.semaphore_wait(barrier, near)

    def send_chunk(j, first):
        own_copy(j, first).start()
        for hop in (2, 3, 1):
            slab_copy(lax.rem(q + hop, SPAN), j, first).start()

    send_chunk(0, True)

    def send_more(j, carry):
        send_chunk(j, False)
        return carry

    lax.fori_loop(1, steps, send_more, 0)

    @pl.when(jnp.logical_not(has_left))
    def _():
        for w in range(SIDE):
            recv[w] = jnp.zeros(recv.shape[1:], BF16)

    @pl.when(jnp.logical_not(has_right))
    def _():
        for w in range(SIDE + SPAN, WIN):
            recv[w] = jnp.zeros(recv.shape[1:], BF16)

    sel_row = lax.broadcasted_iota(jnp.int32, (CELLS, 2 * LANES), 0)
    sel_lane = lax.broadcasted_iota(jnp.int32, (CELLS, 2 * LANES), 1)
    selector = jnp.where(lax.rem(sel_lane, LANES) // ML_RG == sel_row, 1.0, 0.0).astype(BF16)
    contract = (((1,), (1,)), ((), ()))
    edge_lane = lax.rem(lax.broadcasted_iota(jnp.int32, (ML_AZ, SUB, 2 * LANES), 2), LANES)
    from_before = edge_lane >= LANES - TAPS // 2
    sub_row = lax.broadcasted_iota(jnp.int32, (ML_AZ, SUB, 2 * LANES), 1)

    def own_arrive(j, first):
        for w in OWN:
            arrived(w, j, first)

        @pl.when(has_left)
        def _():
            for w in OWN[:SIDE]:
                side_copy(w, j, first).start()

        @pl.when(has_right)
        def _():
            for w in OWN[SIDE:]:
                side_copy(w, j, first).start()

    def far_arrive(j, first):
        @pl.when(has_left)
        def _():
            for w in FAR[:SIDE]:
                arrived(w, j, first)

        @pl.when(has_right)
        def _():
            for w in FAR[SIDE:]:
                arrived(w, j, first)

    def make_after(dates):
        for w in dates:
            value = recv[w, SLOT:SLOT + ML_AZ].astype(F32)
            value = jnp.where(sub_row < SUB - 1, pltpu.roll(value, SUB - 1, 1), 0.0)
            recv[w, SLOT * (steps + 1):SLOT * (steps + 1) + ML_AZ] = value.astype(BF16)

    def make_before(dates):
        for w in dates:
            value = recv[w, SLOT * steps:SLOT * steps + ML_AZ].astype(F32)
            value = jnp.where(sub_row > 0, pltpu.roll(value, 1, 1), 0.0)
            recv[w, 0:ML_AZ] = value.astype(BF16)

    def band_split(dates, j):
        rows = []
        for w in dates:
            here = recv[w, pl.ds(SLOT * (j + 1), ML_AZ)]
            before = recv[w, pl.ds(SLOT * j, ML_AZ)]
            after = recv[w, pl.ds(SLOT * (j + 2), ML_AZ)]
            edge = jnp.where(from_before, before, after)
            rows.append(jnp.concatenate([here, edge], axis=2).reshape(ML_AZ * SUB, 4 * LANES))
        made = jnp.dot(jnp.concatenate(rows, axis=0), mat[...], preferred_element_type=F32)
        return made.astype(BF16).astype(F32).reshape(len(dates), ML_AZ, SUB, 4 * LANES)

    def read(w, j, band, part):
        cols = slice((2 * band + part) * LANES, (2 * band + part + 1) * LANES)
        if w in OWN:
            return [bands_own[j, OWN.index(w), r, :, cols] for r in range(ML_AZ)]
        return [bands_far[FAR.index(w), r, :, cols] for r in range(ML_AZ)]

    def total(terms):
        terms = list(terms)
        while len(terms) > 1:
            terms = [a + b for a, b in zip(terms[::2], terms[1::2])]
        return terms[0]

    def keep_sum(at, value):
        high = value.astype(BF16)
        low = (value - high.astype(F32)).astype(BF16)
        both[at * SUB:at * SUB + SUB, 0:LANES] = high
        both[at * SUB:at * SUB + SUB, LANES:2 * LANES] = low

    def products(dates, pairs, start, j):
        for band in range(2):
            for w in dates:
                re, im = (read(w, j, band, part) for part in range(2))
                keep_sum(ORDER["p", w, band] - start, total([a * a for a in re]) + total([a * a for a in im]))
            for w, k in pairs:
                a_re, a_im = (read(w, j, band, part) for part in range(2))
                b_re, b_im = (read(w + k, j, band, part) for part in range(2))
                re = total([a * b for a, b in zip(a_re, b_re)]) + total([a * b for a, b in zip(a_im, b_im)])
                im = total([a * b for a, b in zip(a_im, b_re)]) - total([a * b for a, b in zip(a_re, b_im)])
                keep_sum(ORDER["r", w, k, band] - start, re)
                keep_sum(ORDER["i", w, k, band] - start, im)

    def own_step(j):
        bands_own[j] = band_split(OWN, j)
        products(OWN, OWN_PAIRS, 0, j)
        red[j, :, 0:OWN_COUNT * SUB] = lax.dot_general(
            selector, both[0:OWN_COUNT * SUB], contract, preferred_element_type=F32
        )

    def far_step(j):
        bands_far[...] = band_split(FAR, j)
        products(FAR, FAR_PAIRS, OWN_COUNT, j)
        red[j, :, OWN_COUNT * SUB:(OWN_COUNT + FAR_COUNT) * SUB] = lax.dot_general(
            selector, both[0:FAR_COUNT * SUB], contract, preferred_element_type=F32
        )

    own_arrive(0, True)
    make_after(OWN)

    def stream(t, carry):
        @pl.when(t < steps)
        def _():
            own_arrive(t, False)

        @pl.when(t == steps - 1)
        def _():
            make_before(OWN)

        @pl.when((t >= 2) & (t < steps + 2))
        def _():
            own_step(lax.rem(t - 1, steps))

        @pl.when(t == 1)
        def _():
            far_arrive(0, True)
            make_after(FAR)

        @pl.when((t >= 2) & (t <= steps))
        def _():
            far_arrive(t - 1, False)

        @pl.when(t == steps)
        def _():
            make_before(FAR)

        @pl.when(t >= 3)
        def _():
            far_step(lax.rem(t - 2, steps))

        return carry

    lax.fori_loop(1, steps + 3, stream, 0)

    def wave(t, carry):
        @pl.when(has_left)
        def _():
            pl.semaphore_signal(wave_sem.at[1], inc=1, device_id={"date": me - SPAN}, device_id_type=mesh_id)

        @pl.when(has_right)
        def _():
            pl.semaphore_signal(wave_sem.at[0], inc=1, device_id={"date": me + SPAN}, device_id_type=mesh_id)

        @pl.when(has_left)
        def _():
            pl.semaphore_wait(wave_sem.at[0], 1)

        @pl.when(has_right)
        def _():
            pl.semaphore_wait(wave_sem.at[1], 1)

        return carry

    lax.fori_loop(1, slabs, wave, 0)

    lane = lax.broadcasted_iota(jnp.int32, (CELLS, LANES), 1)
    for g in range(len(ORDER) // steps):
        rows = [red[j, :, g * LANES:g * LANES + LANES] for j in range(steps)]
        bit = 1
        while bit < steps:
            upper = lax.rem(lane // (SUB * bit), 2) == 1
            turned = list(rows)
            for a in range(steps):
                if a & bit == 0:
                    b = a | bit
                    turned[a] = jnp.where(upper, pltpu.roll(rows[b], SUB * bit, 1), rows[a])
                    turned[b] = jnp.where(upper, rows[b], pltpu.roll(rows[a], LANES - SUB * bit, 1))
            rows = turned
            bit *= 2
        for u in range(steps):
            qty[g * steps + u] = rows[u]

    shape = (SPAN, CELLS, LANES)
    c_id = lax.broadcasted_iota(jnp.int32, shape, 1)
    l_id = lax.broadcasted_iota(jnp.int32, shape, 2)
    last_row = LANES - SUB

    def block_after(x):
        wrap = jnp.where(l_id == LANES - 1, 0.0, pltpu.roll(x, last_row - 1, 2))
        return jnp.where(l_id < last_row, pltpu.roll(x, last_row, 2), wrap)

    def block_before(x):
        wrap = jnp.where(l_id == 0, 0.0, pltpu.roll(x, SUB + 1, 2))
        return jnp.where(l_id >= SUB, pltpu.roll(x, SUB, 2), wrap)

    def box(value):
        prefix = value
        for hop in (1, 2, 4):
            prefix = prefix + jnp.where(c_id >= hop, pltpu.roll(prefix, hop, 1), 0.0)
        whole = jnp.sum(value, axis=1, keepdims=True)
        suffix = whole - prefix + value
        return block_before(suffix) + whole + block_after(prefix)

    def stacked(*keys):
        return jnp.concatenate([qty[ORDER[key]][None] for key in keys], axis=0)

    for k in range(1, SPAN + 1):
        dates = range(first_date(k), first_date(k) + SPAN)
        cr0, cr1 = (stacked(*[("r", w, k, band) for w in dates]) for band in range(2))
        ci0, ci1 = (stacked(*[("i", w, k, band) for w in dates]) for band in range(2))
        ab0, ab1 = (
            stacked(*[("p", w, band) for w in dates]) * stacked(*[("p", w + k, band) for w in dates]) + eps_power
            for band in range(2)
        )
        flag = jnp.concatenate(
            [
                jnp.broadcast_to(
                    recv[w, SLOT + ML_AZ].astype(F32)[k - 1:k, 0:LANES], (CELLS, LANES)
                )[None] for w in dates
            ], axis=0
        )
        weight = flag * 0.5 * ((cr0 * cr0 + ci0 * ci0) / ab0 + (cr1 * cr1 + ci1 * ci1) / ab1)
        phase = split_coef * (ci0 * cr1 - cr0 * ci1) / jnp.sqrt(ab0 * ab1)
        den = box(weight)
        num = box(weight * phase)
        quant[k - 1] = den / (2 * RADIUS + 1)
        quant[SPAN + k - 1] = num / (den + floor_weight)

    kinds = 2 * SPAN
    per = LANES // (SPAN * wide)
    pieces = kinds // per

    def line_copy(target):
        return pltpu.make_async_remote_copy(
            src_ref=msg.at[target], dst_ref=got.at[z],
            send_sem=bsend_sem.at[target], recv_sem=brecv_sem.at[z],
            device_id={"date": target * SPAN + q}, device_id_type=mesh_id,
        )

    def pack_line(target):
        for m in range(pieces):
            value = None
            for u in range(per):
                for g in range(SPAN):
                    at = (u * SPAN + g) * wide
                    shift = lax.rem(at - target * wide + LANES, LANES)
                    moved = pltpu.roll(quant[m * per + u, g], shift, 1)
                    value = moved if value is None else jnp.where(lane >= at, moved, value)
            msg[target, m] = value

    def send_line(target):
        @pl.when(target != z)
        def _():
            line_copy(target).start()

        @pl.when(target == z)
        def _():
            pltpu.make_async_copy(msg.at[z], got.at[z], brecv_sem.at[z]).start()

    def each_line(target, carry):
        pack_line(target)
        send_line(target)
        return carry

    lax.fori_loop(0, slabs, each_line, 0)

    def line_arrive(s, carry):
        pltpu.make_async_copy(got.at[s], got.at[s], brecv_sem.at[s]).wait()
        return carry

    lax.fori_loop(0, slabs, line_arrive, 0)

    regs = n * wide // LANES
    zero = jnp.zeros((CELLS, LANES), F32)

    def gather(kind):
        out = []
        for v in range(regs):
            value = None
            for s in range(v * slabs // regs, (v + 1) * slabs // regs):
                to = s * SPAN * wide - v * LANES
                at = (kind % per) * SPAN * wide
                piece = got[s, kind // per]
                if to != at:
                    piece = pltpu.roll(piece, (to - at) % LANES, 1)
                value = piece if value is None else jnp.where(lane >= to, piece, value)
            out.append(value)
        return out

    def shift(x, dates):
        far, by = divmod(dates * wide, LANES)
        out = []
        for v in range(regs):
            low = x[v + far] if 0 <= v + far < regs else zero
            if by == 0:
                out.append(low)
                continue
            high = x[v + far + 1] if 0 <= v + far + 1 < regs else zero
            out.append(jnp.where(lane < LANES - by, pltpu.roll(low, LANES - by, 1), pltpu.roll(high, LANES - by, 1)))
        return out

    def add(x, y):
        return [a + b for a, b in zip(x, y)]

    ahead, behind = [], []
    wsum = [zero] * regs
    rhs = [zero] * regs
    for k in range(1, SPAN + 1):
        skip = SIDE - first_date(k)
        w = gather(k - 1)
        p = gather(SPAN + k - 1)
        wp = [a * b for a, b in zip(w, p)]
        ahead.append(shift(w, skip))
        behind.append(shift(w, skip - k))
        wsum = add(wsum, add(ahead[-1], behind[-1]))
        rhs = add(rhs, [b - a for a, b in zip(shift(wp, skip), shift(wp, skip - k))])
        if k == 1:
            chain = shift(p, skip)
    hop = 1
    while hop < n:
        chain = add(chain, shift(chain, -hop))
        hop *= 2
    chain = shift(chain, -1)
    rhs = [r + ridge_weight * c for r, c in zip(rhs, chain)]
    inv = [1.0 / (t + ridge_weight) for t in wsum]
    phi = chain
    for sweep in range(ITERS):
        acc = rhs
        for k in range(1, SPAN + 1):
            acc = add(acc, [a * b for a, b in zip(ahead[k - 1], shift(phi, k))])
            acc = add(acc, [a * b for a, b in zip(behind[k - 1], shift(phi, -k))])
        phi = [a * b for a, b in zip(acc, inv)]
    for v in range(regs):
        fin[0, v] = phi[v]
        fin[1, v] = wsum[v]

    def out_copy(target):
        return pltpu.make_async_remote_copy(
            src_ref=pack.at[target], dst_ref=back.at[me],
            send_sem=dsend_sem.at[target], recv_sem=drecv_sem.at[me],
            device_id={"date": target}, device_id_type=mesh_id,
        )

    mine = lane // wide == z
    half = LANES // 2

    def finish(i, carry):
        target = lax.rem(me + i, n)
        v = target * wide // LANES
        at = lax.rem(target * wide, LANES)
        phase = pltpu.roll(fin[0, v], lax.rem(z * wide - at + LANES, LANES), 1)
        weight = pltpu.roll(fin[1, v], lax.rem(z * wide + half - at + LANES, LANES), 1)
        pack[target] = jnp.where(mine, phase, weight)

        @pl.when(i > 0)
        def _():
            out_copy(target).start()

        return carry

    lax.fori_loop(0, n, finish, 0)
    pltpu.make_async_copy(pack.at[me], back.at[me], drecv_sem.at[me]).start()

    def drain_out(i, carry):
        out_copy(lax.rem(me + i, n)).wait_send()
        return carry

    lax.fori_loop(1, n, drain_out, 0)

    def drain_line(s, carry):
        @pl.when(s != z)
        def _():
            line_copy(s).wait_send()
        return carry

    lax.fori_loop(0, slabs, drain_line, 0)

    def drain(j, first):
        for hop in range(1, SPAN):
            slab_copy(lax.rem(q + hop, SPAN), j, first).wait_send()

        @pl.when(has_left)
        def _():
            for w in OWN[:SIDE]:
                side_copy(w, j, first).wait_send()

        @pl.when(has_right)
        def _():
            for w in OWN[SIDE:]:
                side_copy(w, j, first).wait_send()

    drain(0, True)

    def drain_more(j, carry):
        drain(j, False)
        return carry

    lax.fori_loop(1, steps, drain_more, 0)

    def arrive(s, carry):
        pltpu.make_async_copy(back.at[s], back.at[s], drecv_sem.at[s]).wait()
        return carry

    lax.fori_loop(0, n, arrive, 0)

    rows = []
    for kind in range(2):
        place_of = lax.rem(lane + kind * half, LANES) // wide
        for s in range(SPAN):
            value = zero
            for line in range(slabs):
                value = jnp.where(place_of == line, back[line * SPAN + s], value)
            rows.append(pltpu.roll(value, half, 1) if kind else value)
    value = jnp.concatenate(rows, axis=0)
    high = value.astype(BF16)
    rest = value - high.astype(F32)
    middle = rest.astype(BF16)
    low = (rest - middle.astype(F32)).astype(BF16)
    width = out_ref.shape[2]
    place_row = lax.broadcasted_iota(jnp.int32, (LANES, width), 0)
    place_block = lax.broadcasted_iota(jnp.int32, (LANES, width), 1) // CELLS
    place = place_row == lax.rem(place_block, steps) * SUB + place_block // steps
    spread = jnp.dot(
        jnp.concatenate([high, middle, low], axis=0), jnp.where(place, 1.0, 0.0).astype(BF16),
        preferred_element_type=F32,
    )
    count = 2 * SPAN * CELLS
    spread = spread[0:count] + spread[count:2 * count] + spread[2 * count:3 * count]
    spread = spread.reshape(2 * SPAN, CELLS, width)
    s_row = lax.broadcasted_iota(jnp.int32, spread.shape, 1)
    s_col = lax.broadcasted_iota(jnp.int32, spread.shape, 2)
    result = jnp.sum(jnp.where(lax.rem(s_col, CELLS) == s_row, spread, 0.0), axis=1)
    out_ref[0] = result[0:SPAN]
    out_ref[1] = result[SPAN:2 * SPAN]


def local(slc_stack, band_taps, pair_flags):
    n = lax.axis_size("date")
    rows, span = slc_stack.shape[2:]
    steps = span // LANES // SUB
    slabs = n // SPAN
    assert rows == SUB and rows // ML_AZ == SPAN and span == LANES * LANES
    assert n % SPAN == 0 and LANES % slabs == 0 and slabs % SPAN == 0
    wide = LANES // slabs
    pieces = 2 * SPAN * SPAN * wide // LANES
    regs = n * wide // LANES
    tiles = SLOT * (steps + 2)

    vmem = pl.BlockSpec(memory_space=pltpu.VMEM)
    small = lambda *lead: pltpu.VMEM((*lead, CELLS, LANES), F32)
    sem = lambda *lead: pltpu.SemaphoreType.DMA(lead)
    both = pl.pallas_call(
        functools.partial(kernel, n, steps),
        out_shape=jax.ShapeDtypeStruct((2, rows // ML_AZ, span // ML_RG), F32),
        in_specs=[pl.BlockSpec(memory_space=pl.ANY)] * 3,
        out_specs=vmem,
        scratch_shapes=[
            pltpu.VMEM((2, rows, span), BF16),
            pltpu.VMEM((1, SPAN), jnp.int32),
            pltpu.VMEM((2, 2, TAPS), BF16),
            pltpu.VMEM((8, LANES), F32),
            pltpu.VMEM((2 * SUB * SUB, LANES), F32),
            pltpu.VMEM((SPAN, tiles, SUB, 2 * LANES), BF16),
            pltpu.VMEM((WIN, tiles, SUB, 2 * LANES), BF16),
            pltpu.VMEM((4 * LANES, 4 * LANES), BF16),
            pltpu.VMEM((steps, SPAN, ML_AZ, SUB, 4 * LANES), F32),
            pltpu.VMEM((SPAN, ML_AZ, SUB, 4 * LANES), F32),
            pltpu.VMEM((max(OWN_COUNT, FAR_COUNT) * SUB, 2 * LANES), BF16),
            pltpu.VMEM((steps, CELLS, len(ORDER) * SUB), F32),
            small(len(ORDER)),
            small(2 * SPAN, SPAN),
            small(slabs, pieces),
            small(slabs, pieces),
            small(2, regs),
            small(n),
            small(n),
            sem(3), sem(SPAN, steps), sem(WIN, steps), sem(SPAN, steps),
            sem(slabs), sem(slabs), sem(n), sem(n), pltpu.SemaphoreType.REGULAR((2,)),
        ],
        compiler_params=pltpu.CompilerParams(
            collective_id=0, has_side_effects=True, vmem_limit_bytes=60 * 1024 * 1024
        ),
    )(slc_stack, pair_flags, band_taps)
    return both[0:1], both[1:2]


def solution(mesh):
    in_specs = (P("date", None, "group", None), P(), P("date", None))
    out_specs = (P("date", "group", None), P("date", "group", None))
    return jax.shard_map(local, mesh=mesh, in_specs=in_specs, out_specs=out_specs, check_vma=False)
```

time: 45.8 us -> 48.6 us (1.061)
  Pallas kernels: 43.6 us -> 46.4 us
    pallas_call x1, Pallas kernels: 43.6 us -> 46.4 us  [local(): pl.pallas_call(functools.partial(kernel, n, steps), out_shape=jax.ShapeDt...]
where the time goes in v1:
time: 48.6 us; the launch traced here: 48.4 us
  Pallas kernels  46.4 us (95%)
  local copies, waits for them, and re-layouts  1.35 us (3%)
  between operations  0.64 us (1%)
    pallas_call x1, Pallas kernels, local(): pl.pallas_call(functools.partial(kernel, n, steps), out_shape=jax.ShapeDt...  46.4 us
    slice x1, local copies, waits for them, and re-layouts, local(): return (both[0:1], both[1:2])  1.35 us

profile of v1, /device:TPU:0, one launch (start us, length us, event | category | flops | bytes accessed | tf_op | source)
XLA Modules:
  0.0 48.4 jit_solution(14531893391743983304)
XLA Ops:
  0.6 46.4 %shard_map.50 = f32[2,4,1024]{2,1,0:T(4,128)} custom-call(bf16[1,2,16,16384]{3,2,1,0:T(8,128)(2,1)} %slc_hbm.1, s32[1,4]{1,0:T(1,128)} %flags_hbm.1, bf16[2,2,32]{2,1,0:T(2,128)(2,1)} %taps_hbm.1), custom_call_target="tpu_custom_call" | custom-call | tf_op jit(solution)/shard_map/pallas_call | solution.py:653
  47.1 1.3 %fusion = (f32[1,4,1024]{2,1,0:T(4,128)}, f32[1,4,1024]{2,1,0:T(4,128)}) fusion(f32[2,4,1024]{2,1,0:T(4,128)} %shard_map.50), kind=kLoop, calls=%fused_computation | loop fusion | bytes 65536 | tf_op jit(solution)/shard_map/slice | solution.py:685

commit v2 on v1

--- a/solution.py
+++ b/solution.py
@@ -20,6 +20,7 @@
 SIDE = SPAN // 2
 WIN = SPAN + 2 * SIDE
 SLOT = ML_AZ + 1
+LAG = 2
 
 eps_power = 1e-06
 floor_weight = 0.1
@@ -65,7 +66,7 @@
     slc_hbm, flags_hbm, taps_hbm, out_ref,
     slc, flags_in, taps_in, taps_ref, turn, data, recv, mat, bands_own, bands_far, both, red, qty, quant,
     msg, got, fin, pack, back,
-    in_sem, send_sem, recv_sem, fsend_sem, bsend_sem, brecv_sem, dsend_sem, drecv_sem, wave_sem,
+    in_sem, send_sem, recv_sem, wave_sem,
 ):
     me = lax.axis_index("date")
     q = lax.rem(me, SPAN)
@@ -140,12 +141,12 @@
             for i in range(SUB):
                 at = pl.multiple_of((steps * i + j) * LANES, LANES)
                 value = slc[part, :, pl.ds(at, LANES)].astype(F32)
-                turn[pl.ds(part * SUB * SUB + i, SUB, stride=SUB), :] = value
+                turn[(part * SUB + i) * SUB:(part * SUB + i + 1) * SUB, :] = value
         for part in range(2):
             for s in range(SPAN):
                 for r in range(ML_AZ):
-                    row = part * SUB * SUB + (ML_AZ * s + r) * SUB
-                    value = turn[row:row + SUB, :].astype(BF16)
+                    row = part * SUB * SUB + ML_AZ * s + r
+                    value = turn[pl.ds(row, SUB, stride=SUB), :].astype(BF16)
                     data[s, SLOT * (j + 1) + r, :, part * LANES:part * LANES + LANES] = value
         return carry
 
@@ -157,13 +158,13 @@
     def slab_copy(target, j, first):
         return pltpu.make_async_remote_copy(
             src_ref=chunk(data.at[target], j, first), dst_ref=chunk(recv.at[q + SIDE], j, first),
-            send_sem=send_sem.at[target, j], recv_sem=recv_sem.at[q + SIDE, j],
+            send_sem=send_sem.at[0], recv_sem=recv_sem.at[1, j],
             device_id={"date": z * SPAN + target}, device_id_type=mesh_id,
         )
 
     def own_copy(j, first):
         return pltpu.make_async_copy(
-            chunk(data.at[q], j, first), chunk(recv.at[q + SIDE], j, first), recv_sem.at[q + SIDE, j]
+            chunk(data.at[q], j, first), chunk(recv.at[q + SIDE], j, first), recv_sem.at[1, j]
         )
 
     def side_copy(w, j, first):
@@ -171,13 +172,13 @@
         to, device = (w + SPAN, me - SPAN) if go_left else (w - SPAN, me + SPAN)
         return pltpu.make_async_remote_copy(
             src_ref=chunk(recv.at[w], j, first), dst_ref=chunk(recv.at[to], j, first),
-            send_sem=fsend_sem.at[w - SIDE, j], recv_sem=recv_sem.at[to, j],
+            send_sem=send_sem.at[1 if go_left else 2], recv_sem=recv_sem.at[2 if go_left else 0, j],
             device_id={"date": device}, device_id_type=mesh_id,
         )
 
-    def arrived(w, j, first):
-        ref = chunk(recv.at[w], j, first)
-        pltpu.make_async_copy(ref, ref, recv_sem.at[w, j]).wait()
+    def arrived(dates, side, j, first):
+        ref = recv.at[pl.ds(dates[0], len(dates)), pl.ds(SLOT * (j + 1), SLOT if first else ML_AZ)]
+        pltpu.make_async_copy(ref, ref, recv_sem.at[side, j]).wait()
 
     near = SPAN - 1 + has_left.astype(jnp.int32) + has_right.astype(jnp.int32)
     pl.semaphore_wait(barrier, near)
@@ -214,8 +215,7 @@
     sub_row = lax.broadcasted_iota(jnp.int32, (ML_AZ, SUB, 2 * LANES), 1)
 
     def own_arrive(j, first):
-        for w in OWN:
-            arrived(w, j, first)
+        arrived(OWN, 1, j, first)
 
         @pl.when(has_left)
         def _():
@@ -230,13 +230,11 @@
     def far_arrive(j, first):
         @pl.when(has_left)
         def _():
-            for w in FAR[:SIDE]:
-                arrived(w, j, first)
+            arrived(FAR[:SIDE], 0, j, first)
 
         @pl.when(has_right)
         def _():
-            for w in FAR[SIDE:]:
-                arrived(w, j, first)
+            arrived(FAR[SIDE:], 2, j, first)
 
     def make_after(dates):
         for w in dates:
@@ -306,9 +304,35 @@
             selector, both[0:FAR_COUNT * SUB], contract, preferred_element_type=F32
         )
 
+    def wave_signal():
+        @pl.when(has_left)
+        def _():
+            pl.semaphore_signal(wave_sem.at[1], inc=1, device_id={"date": me - SPAN}, device_id_type=mesh_id)
+
+        @pl.when(has_right)
+        def _():
+            pl.semaphore_signal(wave_sem.at[0], inc=1, device_id={"date": me + SPAN}, device_id_type=mesh_id)
+
+    def wave(t, carry):
+        @pl.when(has_left)
+        def _():
+            pl.semaphore_wait(wave_sem.at[0], 1)
+
+        @pl.when(has_right)
+        def _():
+            pl.semaphore_wait(wave_sem.at[1], 1)
+
+        @pl.when(t < slabs - 1)
+        def _():
+            wave_signal()
+
+        return carry
+
     own_arrive(0, True)
     make_after(OWN)
 
+    wave_signal()
+
     def stream(t, carry):
         @pl.when(t < steps)
         def _():
@@ -318,51 +342,35 @@
         def _():
             make_before(OWN)
 
+        @pl.when(t < slabs)
+        def _():
+            wave(t, 0)
+
         @pl.when((t >= 2) & (t < steps + 2))
         def _():
             own_step(lax.rem(t - 1, steps))
 
-        @pl.when(t == 1)
+        @pl.when(t == LAG)
         def _():
             far_arrive(0, True)
             make_after(FAR)
 
-        @pl.when((t >= 2) & (t <= steps))
-        def _():
-            far_arrive(t - 1, False)
-
-        @pl.when(t == steps)
+        @pl.when((t > LAG) & (t < steps + LAG))
+        def _():
+            far_arrive(t - LAG, False)
+
+        @pl.when(t == steps + LAG - 1)
         def _():
             make_before(FAR)
 
-        @pl.when(t >= 3)
-        def _():
-            far_step(lax.rem(t - 2, steps))
+        @pl.when(t >= LAG + 2)
+        def _():
+            far_step(lax.rem(t - LAG - 1, steps))
 
         return carry
 
-    lax.fori_loop(1, steps + 3, stream, 0)
-
-    def wave(t, carry):
-        @pl.when(has_left)
-        def _():
-            pl.semaphore_signal(wave_sem.at[1], inc=1, device_id={"date": me - SPAN}, device_id_type=mesh_id)
-
-        @pl.when(has_right)
-        def _():
-            pl.semaphore_signal(wave_sem.at[0], inc=1, device_id={"date": me + SPAN}, device_id_type=mesh_id)
-
-        @pl.when(has_left)
-        def _():
-            pl.semaphore_wait(wave_sem.at[0], 1)
-
-        @pl.when(has_right)
-        def _():
-            pl.semaphore_wait(wave_sem.at[1], 1)
-
-        return carry
-
-    lax.fori_loop(1, slabs, wave, 0)
+    lax.fori_loop(1, steps + LAG + 2, stream, 0)
+    lax.fori_loop(steps + LAG + 2, slabs, wave, 0)
 
     lane = lax.broadcasted_iota(jnp.int32, (CELLS, LANES), 1)
     for g in range(len(ORDER) // steps):
@@ -434,7 +442,7 @@
     def line_copy(target):
         return pltpu.make_async_remote_copy(
             src_ref=msg.at[target], dst_ref=got.at[z],
-            send_sem=bsend_sem.at[target], recv_sem=brecv_sem.at[z],
+            send_sem=send_sem.at[3], recv_sem=recv_sem.at[0, steps],
             device_id={"date": target * SPAN + q}, device_id_type=mesh_id,
         )
 
@@ -456,20 +464,20 @@
 
         @pl.when(target == z)
         def _():
-            pltpu.make_async_copy(msg.at[z], got.at[z], brecv_sem.at[z]).start()
+            pltpu.make_async_copy(msg.at[z], got.at[z], recv_sem.at[0, steps]).start()
 
     def each_line(target, carry):
         pack_line(target)
         send_line(target)
         return carry
 
-    lax.fori_loop(0, slabs, each_line, 0)
-
-    def line_arrive(s, carry):
-        pltpu.make_async_copy(got.at[s], got.at[s], brecv_sem.at[s]).wait()
-        return carry
-
-    lax.fori_loop(0, slabs, line_arrive, 0)
+    if slabs <= steps:
+        for target in range(slabs):
+            each_line(target, 0)
+    else:
+        lax.fori_loop(0, slabs, each_line, 0)
+
+    pltpu.make_async_copy(got, got, recv_sem.at[0, steps]).wait()
 
     regs = n * wide // LANES
     zero = jnp.zeros((CELLS, LANES), F32)
@@ -531,78 +539,62 @@
             acc = add(acc, [a * b for a, b in zip(ahead[k - 1], shift(phi, k))])
             acc = add(acc, [a * b for a, b in zip(behind[k - 1], shift(phi, -k))])
         phi = [a * b for a, b in zip(acc, inv)]
-    for v in range(regs):
-        fin[0, v] = phi[v]
-        fin[1, v] = wsum[v]
 
     def out_copy(target):
         return pltpu.make_async_remote_copy(
             src_ref=pack.at[target], dst_ref=back.at[me],
-            send_sem=dsend_sem.at[target], recv_sem=drecv_sem.at[me],
+            send_sem=send_sem.at[4], recv_sem=recv_sem.at[0, steps + 1],
             device_id={"date": target}, device_id_type=mesh_id,
         )
 
     mine = lane // wide == z
     half = LANES // 2
 
-    def finish(i, carry):
-        target = lax.rem(me + i, n)
-        v = target * wide // LANES
-        at = lax.rem(target * wide, LANES)
-        phase = pltpu.roll(fin[0, v], lax.rem(z * wide - at + LANES, LANES), 1)
-        weight = pltpu.roll(fin[1, v], lax.rem(z * wide + half - at + LANES, LANES), 1)
+    def finish(target, phase, weight, at):
+        phase = pltpu.roll(phase, lax.rem(LANES - at, LANES), 1)
+        weight = pltpu.roll(weight, lax.rem(LANES - at, LANES), 1)
         pack[target] = jnp.where(mine, phase, weight)
 
-        @pl.when(i > 0)
+        @pl.when(target != me)
         def _():
             out_copy(target).start()
 
-        return carry
-
-    lax.fori_loop(0, n, finish, 0)
-    pltpu.make_async_copy(pack.at[me], back.at[me], drecv_sem.at[me]).start()
-
-    def drain_out(i, carry):
-        out_copy(lax.rem(me + i, n)).wait_send()
-        return carry
-
-    lax.fori_loop(1, n, drain_out, 0)
-
-    def drain_line(s, carry):
-        @pl.when(s != z)
-        def _():
-            line_copy(s).wait_send()
-        return carry
-
-    lax.fori_loop(0, slabs, drain_line, 0)
-
-    def drain(j, first):
-        for hop in range(1, SPAN):
-            slab_copy(lax.rem(q + hop, SPAN), j, first).wait_send()
-
-        @pl.when(has_left)
-        def _():
-            for w in OWN[:SIDE]:
-                side_copy(w, j, first).wait_send()
-
-        @pl.when(has_right)
-        def _():
-            for w in OWN[SIDE:]:
-                side_copy(w, j, first).wait_send()
-
-    drain(0, True)
-
-    def drain_more(j, carry):
-        drain(j, False)
-        return carry
-
-    lax.fori_loop(1, steps, drain_more, 0)
-
-    def arrive(s, carry):
-        pltpu.make_async_copy(back.at[s], back.at[s], drecv_sem.at[s]).wait()
-        return carry
-
-    lax.fori_loop(0, n, arrive, 0)
+    phi = [pltpu.roll(x, z * wide, 1) for x in phi]
+    wsum = [pltpu.roll(x, lax.rem(z * wide + half, LANES), 1) for x in wsum]
+    if n <= 2 * SUB:
+        for target in range(n):
+            v = target * wide // LANES
+            finish(target, phi[v], wsum[v], target * wide % LANES)
+    else:
+        for v in range(regs):
+            fin[0, v] = phi[v]
+            fin[1, v] = wsum[v]
+
+        def finish_more(target, carry):
+            v = target * wide // LANES
+            finish(target, fin[0, v], fin[1, v], lax.rem(target * wide, LANES))
+            return carry
+
+        lax.fori_loop(0, n, finish_more, 0)
+    pltpu.make_async_copy(pack.at[me], back.at[me], recv_sem.at[0, steps + 1]).start()
+
+    def drain(ref, sem):
+        pltpu.make_async_copy(ref, ref, sem).wait()
+
+    tiles = SLOT + ML_AZ * (steps - 1)
+    drain(data.at[pl.ds(0, SPAN - 1), pl.ds(0, tiles)], send_sem.at[0])
+
+    @pl.when(has_left)
+    def _():
+        drain(data.at[pl.ds(0, SIDE), pl.ds(0, tiles)], send_sem.at[1])
+
+    @pl.when(has_right)
+    def _():
+        drain(data.at[pl.ds(0, SIDE), pl.ds(0, tiles)], send_sem.at[2])
+
+    drain(msg.at[pl.ds(0, slabs - 1)], send_sem.at[3])
+    drain(back, recv_sem.at[0, steps + 1])
+    drain(pack.at[pl.ds(0, n - 1)], send_sem.at[4])
 
     rows = []
     for kind in range(2):
@@ -675,8 +667,7 @@
             small(2, regs),
             small(n),
             small(n),
-            sem(3), sem(SPAN, steps), sem(WIN, steps), sem(SPAN, steps),
-            sem(slabs), sem(slabs), sem(n), sem(n), pltpu.SemaphoreType.REGULAR((2,)),
+            sem(3), sem(5), sem(3, steps + 2), pltpu.SemaphoreType.REGULAR((2,)),
         ],
         compiler_params=pltpu.CompilerParams(
             collective_id=0, has_side_effects=True, vmem_limit_bytes=60 * 1024 * 1024

time: 48.6 us -> 39.4 us (0.81)
  Pallas kernels: 46.4 us -> 37.2 us
    pallas_call x1, Pallas kernels: 46.4 us -> 37.2 us  [local(): pl.pallas_call(functools.partial(kernel, n, steps), out_shape=jax.ShapeDt...]
where the time goes in v2:
time: 39.4 us; the launch traced here: 39.2 us
  Pallas kernels  37.2 us (94%)
  local copies, waits for them, and re-layouts  1.35 us (3%)
  between operations  0.64 us (2%)
    pallas_call x1, Pallas kernels, local(): pl.pallas_call(functools.partial(kernel, n, steps), out_shape=jax.ShapeDt...  37.2 us
    slice x1, local copies, waits for them, and re-layouts, local(): return (both[0:1], both[1:2])  1.35 us

profile of v2, /device:TPU:0, one launch (start us, length us, event | category | flops | bytes accessed | tf_op | source)
XLA Modules:
  0.0 39.2 jit_solution(17406161973940812617)
XLA Ops:
  0.6 37.2 %shard_map.50 = f32[2,4,1024]{2,1,0:T(4,128)} custom-call(bf16[1,2,16,16384]{3,2,1,0:T(8,128)(2,1)} %slc_hbm.1, s32[1,4]{1,0:T(1,128)} %flags_hbm.1, bf16[2,2,32]{2,1,0:T(2,128)(2,1)} %taps_hbm.1), custom_call_target="tpu_custom_call" | custom-call | tf_op jit(solution)/shard_map/pallas_call | solution.py:645
  37.9 1.3 %fusion = (f32[1,4,1024]{2,1,0:T(4,128)}, f32[1,4,1024]{2,1,0:T(4,128)}) fusion(f32[2,4,1024]{2,1,0:T(4,128)} %shard_map.50), kind=kLoop, calls=%fused_computation | loop fusion | bytes 65536 | tf_op jit(solution)/shard_map/slice | solution.py:676

commit v3 on v2

--- a/solution.py
+++ b/solution.py
@@ -43,36 +43,32 @@
 FAR_PAIRS = [p for p in PAIRS if p not in OWN_PAIRS]
 
 
-def listing():
-    order = {}
-    for dates, pairs in ((OWN, OWN_PAIRS), (FAR, FAR_PAIRS)):
-        for w in dates:
-            for band in range(2):
-                order["p", w, band] = len(order)
-        for w, k in pairs:
-            for band in range(2):
-                order["r", w, k, band] = len(order)
-                order["i", w, k, band] = len(order)
-    return order
-
-
-ORDER = listing()
-OWN_COUNT = 2 * SPAN + 4 * len(OWN_PAIRS)
-FAR_COUNT = 2 * SPAN + 4 * len(FAR_PAIRS)
+HALVES = 2
+GROUP = SPAN * SPAN // HALVES
+
+
+def pair_slot(imag, band, w, k):
+    return ((2 * band + imag) * HALVES + (k - 1) // HALVES) * GROUP + (k - 1) % HALVES * SPAN + w - first_date(k)
+
+
+def power_slot(band, w):
+    return 4 * HALVES * GROUP + band * WIN + w
+
+
+SLOTS = power_slot(1, WIN - 1) + 1
 
 
 def kernel(
     n, steps,
     slc_hbm, flags_hbm, taps_hbm, out_ref,
-    slc, flags_in, taps_in, taps_ref, turn, data, recv, mat, bands_own, bands_far, both, red, qty, quant,
-    msg, got, fin, pack, back,
+    slc, flags_in, taps_in, taps_ref, turn, data, recv, mat, bands_own, bands_far, both, red, quant,
+    got, pack, back,
     in_sem, send_sem, recv_sem, wave_sem,
 ):
     me = lax.axis_index("date")
     q = lax.rem(me, SPAN)
     z = me // SPAN
     slabs = n // SPAN
-    wide = LANES // slabs
     has_left = z > 0
     has_right = z < slabs - 1
     mesh_id = pl.DeviceIdType.MESH
@@ -271,38 +267,33 @@
             terms = [a + b for a, b in zip(terms[::2], terms[1::2])]
         return terms[0]
 
-    def keep_sum(at, value):
+    def keep_sum(j, at, value):
         high = value.astype(BF16)
         low = (value - high.astype(F32)).astype(BF16)
-        both[at * SUB:at * SUB + SUB, 0:LANES] = high
-        both[at * SUB:at * SUB + SUB, LANES:2 * LANES] = low
-
-    def products(dates, pairs, start, j):
+        both[j, at * SUB:at * SUB + SUB, 0:LANES] = high
+        both[j, at * SUB:at * SUB + SUB, LANES:2 * LANES] = low
+
+    def products(dates, pairs, j):
         for band in range(2):
             for w in dates:
                 re, im = (read(w, j, band, part) for part in range(2))
-                keep_sum(ORDER["p", w, band] - start, total([a * a for a in re]) + total([a * a for a in im]))
+                keep_sum(j, power_slot(band, w), total([a * a for a in re]) + total([a * a for a in im]))
             for w, k in pairs:
                 a_re, a_im = (read(w, j, band, part) for part in range(2))
                 b_re, b_im = (read(w + k, j, band, part) for part in range(2))
                 re = total([a * b for a, b in zip(a_re, b_re)]) + total([a * b for a, b in zip(a_im, b_im)])
                 im = total([a * b for a, b in zip(a_im, b_re)]) - total([a * b for a, b in zip(a_re, b_im)])
-                keep_sum(ORDER["r", w, k, band] - start, re)
-                keep_sum(ORDER["i", w, k, band] - start, im)
+                keep_sum(j, pair_slot(0, band, w, k), re)
+                keep_sum(j, pair_slot(1, band, w, k), im)
 
     def own_step(j):
         bands_own[j] = band_split(OWN, j)
-        products(OWN, OWN_PAIRS, 0, j)
-        red[j, :, 0:OWN_COUNT * SUB] = lax.dot_general(
-            selector, both[0:OWN_COUNT * SUB], contract, preferred_element_type=F32
-        )
+        products(OWN, OWN_PAIRS, j)
 
     def far_step(j):
         bands_far[...] = band_split(FAR, j)
-        products(FAR, FAR_PAIRS, OWN_COUNT, j)
-        red[j, :, OWN_COUNT * SUB:(OWN_COUNT + FAR_COUNT) * SUB] = lax.dot_general(
-            selector, both[0:FAR_COUNT * SUB], contract, preferred_element_type=F32
-        )
+        products(FAR, FAR_PAIRS, j)
+        red[j] = lax.dot_general(selector, both[j], contract, preferred_element_type=F32)
 
     def wave_signal():
         @pl.when(has_left)
@@ -372,35 +363,10 @@
     lax.fori_loop(1, steps + LAG + 2, stream, 0)
     lax.fori_loop(steps + LAG + 2, slabs, wave, 0)
 
-    lane = lax.broadcasted_iota(jnp.int32, (CELLS, LANES), 1)
-    for g in range(len(ORDER) // steps):
-        rows = [red[j, :, g * LANES:g * LANES + LANES] for j in range(steps)]
-        bit = 1
-        while bit < steps:
-            upper = lax.rem(lane // (SUB * bit), 2) == 1
-            turned = list(rows)
-            for a in range(steps):
-                if a & bit == 0:
-                    b = a | bit
-                    turned[a] = jnp.where(upper, pltpu.roll(rows[b], SUB * bit, 1), rows[a])
-                    turned[b] = jnp.where(upper, rows[b], pltpu.roll(rows[a], LANES - SUB * bit, 1))
-            rows = turned
-            bit *= 2
-        for u in range(steps):
-            qty[g * steps + u] = rows[u]
-
-    shape = (SPAN, CELLS, LANES)
+    shape = (steps, CELLS, LANES)
     c_id = lax.broadcasted_iota(jnp.int32, shape, 1)
     l_id = lax.broadcasted_iota(jnp.int32, shape, 2)
-    last_row = LANES - SUB
-
-    def block_after(x):
-        wrap = jnp.where(l_id == LANES - 1, 0.0, pltpu.roll(x, last_row - 1, 2))
-        return jnp.where(l_id < last_row, pltpu.roll(x, last_row, 2), wrap)
-
-    def block_before(x):
-        wrap = jnp.where(l_id == 0, 0.0, pltpu.roll(x, SUB + 1, 2))
-        return jnp.where(l_id >= SUB, pltpu.roll(x, SUB, 2), wrap)
+    i_id = lax.rem(l_id, SUB)
 
     def box(value):
         prefix = value
@@ -408,96 +374,107 @@
             prefix = prefix + jnp.where(c_id >= hop, pltpu.roll(prefix, hop, 1), 0.0)
         whole = jnp.sum(value, axis=1, keepdims=True)
         suffix = whole - prefix + value
-        return block_before(suffix) + whole + block_after(prefix)
-
-    def stacked(*keys):
-        return jnp.concatenate([qty[ORDER[key]][None] for key in keys], axis=0)
-
-    for k in range(1, SPAN + 1):
-        dates = range(first_date(k), first_date(k) + SPAN)
-        cr0, cr1 = (stacked(*[("r", w, k, band) for w in dates]) for band in range(2))
-        ci0, ci1 = (stacked(*[("i", w, k, band) for w in dates]) for band in range(2))
+        first = jnp.where(i_id[0:1] > 0, pltpu.roll(suffix[steps - 1:steps], 1, 2), 0.0)
+        last = jnp.where(i_id[0:1] < SUB - 1, pltpu.roll(prefix[0:1], LANES - 1, 2), 0.0)
+        before = jnp.concatenate([first, suffix[0:steps - 1]], axis=0)
+        after = jnp.concatenate([prefix[1:steps], last], axis=0)
+        return before + whole + after
+
+    def register(at):
+        return red[:, :, at * LANES:at * LANES + LANES]
+
+    lane = lax.broadcasted_iota(jnp.int32, (CELLS, LANES), 1)
+    span_lanes = SPAN * SUB
+
+    def aligned(value, ks, partner):
+        parts = []
+        for at, k in enumerate(ks):
+            w = first_date(k) + (k if partner else 0)
+            move = (at * SPAN - w) * SUB % LANES
+            parts.append(pltpu.roll(value, move, 2) if move else value)
+        return jnp.where(l_id < span_lanes, parts[0], parts[1])
+
+    for h in range(HALVES):
+        ks = (HALVES * h + 1, HALVES * h + 2)
+        cr0, ci0, cr1, ci1 = (register(m * HALVES + h) for m in range(4))
         ab0, ab1 = (
-            stacked(*[("p", w, band) for w in dates]) * stacked(*[("p", w + k, band) for w in dates]) + eps_power
-            for band in range(2)
+            aligned(power, ks, False) * aligned(power, ks, True) + eps_power
+            for power in (register(4 * HALVES), register(4 * HALVES + 1))
         )
-        flag = jnp.concatenate(
-            [
-                jnp.broadcast_to(
-                    recv[w, SLOT + ML_AZ].astype(F32)[k - 1:k, 0:LANES], (CELLS, LANES)
-                )[None] for w in dates
-            ], axis=0
-        )
-        weight = flag * 0.5 * ((cr0 * cr0 + ci0 * ci0) / ab0 + (cr1 * cr1 + ci1 * ci1) / ab1)
+        flag = jnp.zeros((CELLS, LANES), F32)
+        for at, k in enumerate(ks):
+            for g in range(SPAN):
+                one = recv[first_date(k) + g, SLOT + ML_AZ].astype(F32)[k - 1:k, 0:LANES]
+                flag = jnp.where(lane >= (at * SPAN + g) * SUB, jnp.broadcast_to(one, flag.shape), flag)
+        weight = flag[None] * 0.5 * ((cr0 * cr0 + ci0 * ci0) / ab0 + (cr1 * cr1 + ci1 * ci1) / ab1)
         phase = split_coef * (ci0 * cr1 - cr0 * ci1) / jnp.sqrt(ab0 * ab1)
         den = box(weight)
         num = box(weight * phase)
-        quant[k - 1] = den / (2 * RADIUS + 1)
-        quant[SPAN + k - 1] = num / (den + floor_weight)
-
-    kinds = 2 * SPAN
-    per = LANES // (SPAN * wide)
-    pieces = kinds // per
-
-    def line_copy(target):
+        quant[:, h] = den / (2 * RADIUS + 1)
+        quant[:, HALVES + h] = num / (den + floor_weight)
+
+    share = got.shape[1]
+    workers = steps // share
+    base = (slabs - workers) // 2
+    is_worker = (z >= base) & (z < base + workers)
+
+    def line_copy(u):
         return pltpu.make_async_remote_copy(
-            src_ref=msg.at[target], dst_ref=got.at[z],
+            src_ref=quant.at[pl.ds(u * share, share)], dst_ref=got.at[z],
             send_sem=send_sem.at[3], recv_sem=recv_sem.at[0, steps],
-            device_id={"date": target * SPAN + q}, device_id_type=mesh_id,
+            device_id={"date": (base + u) * SPAN + q}, device_id_type=mesh_id,
         )
 
-    def pack_line(target):
-        for m in range(pieces):
-            value = None
-            for u in range(per):
-                for g in range(SPAN):
-                    at = (u * SPAN + g) * wide
-                    shift = lax.rem(at - target * wide + LANES, LANES)
-                    moved = pltpu.roll(quant[m * per + u, g], shift, 1)
-                    value = moved if value is None else jnp.where(lane >= at, moved, value)
-            msg[target, m] = value
-
-    def send_line(target):
-        @pl.when(target != z)
-        def _():
-            line_copy(target).start()
-
-        @pl.when(target == z)
-        def _():
-            pltpu.make_async_copy(msg.at[z], got.at[z], recv_sem.at[0, steps]).start()
-
-    def each_line(target, carry):
-        pack_line(target)
-        send_line(target)
-        return carry
-
-    if slabs <= steps:
-        for target in range(slabs):
-            each_line(target, 0)
-    else:
-        lax.fori_loop(0, slabs, each_line, 0)
-
-    pltpu.make_async_copy(got, got, recv_sem.at[0, steps]).wait()
-
-    regs = n * wide // LANES
+    for u in range(workers):
+        @pl.when(z != base + u)
+        def _():
+            line_copy(u).start()
+
+        @pl.when(z == base + u)
+        def _():
+            pltpu.make_async_copy(
+                quant.at[pl.ds(u * share, share)], got.at[z], recv_sem.at[0, steps]
+            ).start()
+
+    def out_copy(target):
+        return pltpu.make_async_remote_copy(
+            src_ref=pack.at[target], dst_ref=back.at[(z - base) * SPAN + q],
+            send_sem=send_sem.at[4], recv_sem=recv_sem.at[0, steps + 1],
+            device_id={"date": target}, device_id_type=mesh_id,
+        )
+
+    def turned(rows):
+        rows = list(rows)
+        bit = 1
+        while bit < len(rows):
+            upper = lax.rem(lane // (SUB * bit), 2) == 1
+            for a in range(len(rows)):
+                if a & bit == 0:
+                    low, high = rows[a], rows[a | bit]
+                    rows[a] = jnp.where(upper, pltpu.roll(high, SUB * bit, 1), low)
+                    rows[a | bit] = jnp.where(upper, high, pltpu.roll(low, LANES - SUB * bit, 1))
+            bit *= 2
+        return rows
+
+    regs = n * SUB // LANES
     zero = jnp.zeros((CELLS, LANES), F32)
-
-    def gather(kind):
+    per = LANES // span_lanes
+
+    def gather(jj, kind, k):
         out = []
+        at = (k - 1) % HALVES * span_lanes
         for v in range(regs):
             value = None
-            for s in range(v * slabs // regs, (v + 1) * slabs // regs):
-                to = s * SPAN * wide - v * LANES
-                at = (kind % per) * SPAN * wide
-                piece = got[s, kind // per]
-                if to != at:
-                    piece = pltpu.roll(piece, (to - at) % LANES, 1)
-                value = piece if value is None else jnp.where(lane >= to, piece, value)
+            for m in range(per):
+                piece = got[v * per + m, jj, kind * HALVES + (k - 1) // HALVES]
+                move = (m * span_lanes - at) % LANES
+                piece = pltpu.roll(piece, move, 1) if move else piece
+                value = piece if value is None else jnp.where(lane >= m * span_lanes, piece, value)
             out.append(value)
         return out
 
     def shift(x, dates):
-        far, by = divmod(dates * wide, LANES)
+        far, by = divmod(dates * SUB, LANES)
         out = []
         for v in range(regs):
             low = x[v + far] if 0 <= v + far < regs else zero
@@ -505,78 +482,66 @@
                 out.append(low)
                 continue
             high = x[v + far + 1] if 0 <= v + far + 1 < regs else zero
-            out.append(jnp.where(lane < LANES - by, pltpu.roll(low, LANES - by, 1), pltpu.roll(high, LANES - by, 1)))
+            out.append(pltpu.roll(jnp.where(lane >= by, low, high), LANES - by, 1))
         return out
 
     def add(x, y):
         return [a + b for a, b in zip(x, y)]
 
-    ahead, behind = [], []
-    wsum = [zero] * regs
-    rhs = [zero] * regs
-    for k in range(1, SPAN + 1):
-        skip = SIDE - first_date(k)
-        w = gather(k - 1)
-        p = gather(SPAN + k - 1)
-        wp = [a * b for a, b in zip(w, p)]
-        ahead.append(shift(w, skip))
-        behind.append(shift(w, skip - k))
-        wsum = add(wsum, add(ahead[-1], behind[-1]))
-        rhs = add(rhs, [b - a for a, b in zip(shift(wp, skip), shift(wp, skip - k))])
-        if k == 1:
-            chain = shift(p, skip)
-    hop = 1
-    while hop < n:
-        chain = add(chain, shift(chain, -hop))
-        hop *= 2
-    chain = shift(chain, -1)
-    rhs = [r + ridge_weight * c for r, c in zip(rhs, chain)]
-    inv = [1.0 / (t + ridge_weight) for t in wsum]
-    phi = chain
-    for sweep in range(ITERS):
-        acc = rhs
+    def relax(jj):
+        ahead, behind = [], []
+        wsum = [zero] * regs
+        rhs = [zero] * regs
         for k in range(1, SPAN + 1):
-            acc = add(acc, [a * b for a, b in zip(ahead[k - 1], shift(phi, k))])
-            acc = add(acc, [a * b for a, b in zip(behind[k - 1], shift(phi, -k))])
-        phi = [a * b for a, b in zip(acc, inv)]
-
-    def out_copy(target):
-        return pltpu.make_async_remote_copy(
-            src_ref=pack.at[target], dst_ref=back.at[me],
-            send_sem=send_sem.at[4], recv_sem=recv_sem.at[0, steps + 1],
-            device_id={"date": target}, device_id_type=mesh_id,
-        )
-
-    mine = lane // wide == z
+            skip = SIDE - first_date(k)
+            w = gather(jj, 0, k)
+            p = gather(jj, 1, k)
+            wp = [a * b for a, b in zip(w, p)]
+            ahead.append(shift(w, skip))
+            behind.append(shift(w, skip - k))
+            wsum = add(wsum, add(ahead[-1], behind[-1]))
+            rhs = add(rhs, [b - a for a, b in zip(shift(wp, skip), shift(wp, skip - k))])
+            if k == 1:
+                chain = shift(p, skip)
+        hop = 1
+        while hop < n:
+            chain = add(chain, shift(chain, -hop))
+            hop *= 2
+        chain = shift(chain, -1)
+        rhs = [r + ridge_weight * c for r, c in zip(rhs, chain)]
+        inv = [1.0 / (t + ridge_weight) for t in wsum]
+        phi = chain
+        for sweep in range(ITERS):
+            acc = rhs
+            for k in range(1, SPAN + 1):
+                acc = add(acc, [a * b for a, b in zip(ahead[k - 1], shift(phi, k))])
+                acc = add(acc, [a * b for a, b in zip(behind[k - 1], shift(phi, -k))])
+            phi = [a * b for a, b in zip(acc, inv)]
+        return phi, wsum
+
     half = LANES // 2
-
-    def finish(target, phase, weight, at):
-        phase = pltpu.roll(phase, lax.rem(LANES - at, LANES), 1)
-        weight = pltpu.roll(weight, lax.rem(LANES - at, LANES), 1)
-        pack[target] = jnp.where(mine, phase, weight)
-
-        @pl.when(target != me)
-        def _():
-            out_copy(target).start()
-
-    phi = [pltpu.roll(x, z * wide, 1) for x in phi]
-    wsum = [pltpu.roll(x, lax.rem(z * wide + half, LANES), 1) for x in wsum]
-    if n <= 2 * SUB:
-        for target in range(n):
-            v = target * wide // LANES
-            finish(target, phi[v], wsum[v], target * wide % LANES)
-    else:
+    ranks = LANES // SUB
+
+    @pl.when(is_worker)
+    def _():
+        pltpu.make_async_copy(got, got, recv_sem.at[0, steps]).wait()
+        made = [relax(jj) for jj in range(share)]
         for v in range(regs):
-            fin[0, v] = phi[v]
-            fin[1, v] = wsum[v]
-
-        def finish_more(target, carry):
-            v = target * wide // LANES
-            finish(target, fin[0, v], fin[1, v], lax.rem(target * wide, LANES))
+            rows = [zero] * ranks
+            for jj in range(share):
+                for kind in range(2):
+                    rows[kind * ranks // 2 + jj] = made[jj][kind][v]
+            for d, value in enumerate(turned(rows)):
+                pack[v * ranks + d] = value
+
+        def send_back(i, carry):
+            out_copy(lax.rem(me + i, n)).start()
             return carry
 
-        lax.fori_loop(0, n, finish_more, 0)
-    pltpu.make_async_copy(pack.at[me], back.at[me], recv_sem.at[0, steps + 1]).start()
+        lax.fori_loop(1, n, send_back, 0)
+        pltpu.make_async_copy(
+            pack.at[me], back.at[(z - base) * SPAN + q], recv_sem.at[0, steps + 1]
+        ).start()
 
     def drain(ref, sem):
         pltpu.make_async_copy(ref, ref, sem).wait()
@@ -592,18 +557,28 @@
     def _():
         drain(data.at[pl.ds(0, SIDE), pl.ds(0, tiles)], send_sem.at[2])
 
-    drain(msg.at[pl.ds(0, slabs - 1)], send_sem.at[3])
+    drain(quant.at[pl.ds(0, steps - share)], send_sem.at[3])
+
+    @pl.when(jnp.logical_not(is_worker))
+    def _():
+        drain(quant.at[pl.ds(0, share)], send_sem.at[3])
+
     drain(back, recv_sem.at[0, steps + 1])
-    drain(pack.at[pl.ds(0, n - 1)], send_sem.at[4])
+
+    @pl.when(is_worker)
+    def _():
+        drain(pack.at[pl.ds(0, n - 1)], send_sem.at[4])
 
     rows = []
     for kind in range(2):
-        place_of = lax.rem(lane + kind * half, LANES) // wide
         for s in range(SPAN):
-            value = zero
-            for line in range(slabs):
-                value = jnp.where(place_of == line, back[line * SPAN + s], value)
-            rows.append(pltpu.roll(value, half, 1) if kind else value)
+            value = None
+            for u in range(workers):
+                move = (u * share * SUB - kind * half) % LANES
+                piece = back[u * SPAN + s]
+                piece = pltpu.roll(piece, move, 1) if move else piece
+                value = piece if value is None else jnp.where(lane >= u * share * SUB, piece, value)
+            rows.append(value)
     value = jnp.concatenate(rows, axis=0)
     high = value.astype(BF16)
     rest = value - high.astype(F32)
@@ -633,10 +608,10 @@
     steps = span // LANES // SUB
     slabs = n // SPAN
     assert rows == SUB and rows // ML_AZ == SPAN and span == LANES * LANES
-    assert n % SPAN == 0 and LANES % slabs == 0 and slabs % SPAN == 0
-    wide = LANES // slabs
-    pieces = 2 * SPAN * SPAN * wide // LANES
-    regs = n * wide // LANES
+    assert n % (LANES // SUB) == 0 and steps == LANES // SUB
+    workers = 1
+    while 2 * workers <= min(steps, slabs // 2):
+        workers *= 2
     tiles = SLOT * (steps + 2)
 
     vmem = pl.BlockSpec(memory_space=pltpu.VMEM)
@@ -658,15 +633,12 @@
             pltpu.VMEM((4 * LANES, 4 * LANES), BF16),
             pltpu.VMEM((steps, SPAN, ML_AZ, SUB, 4 * LANES), F32),
             pltpu.VMEM((SPAN, ML_AZ, SUB, 4 * LANES), F32),
-            pltpu.VMEM((max(OWN_COUNT, FAR_COUNT) * SUB, 2 * LANES), BF16),
-            pltpu.VMEM((steps, CELLS, len(ORDER) * SUB), F32),
-            small(len(ORDER)),
-            small(2 * SPAN, SPAN),
-            small(slabs, pieces),
-            small(slabs, pieces),
-            small(2, regs),
+            pltpu.VMEM((steps, SLOTS * SUB, 2 * LANES), BF16),
+            pltpu.VMEM((steps, CELLS, SLOTS * SUB), F32),
+            small(steps, 2 * HALVES),
+            small(slabs, steps // workers, 2 * HALVES),
             small(n),
-            small(n),
+            small(workers * SPAN),
             sem(3), sem(5), sem(3, steps + 2), pltpu.SemaphoreType.REGULAR((2,)),
         ],
         compiler_params=pltpu.CompilerParams(

time: 39.4 us -> 38.5 us (0.977)
  Pallas kernels: 37.2 us -> 36.2 us
    pallas_call x1, Pallas kernels: 37.2 us -> 36.2 us  [local(): pl.pallas_call(functools.partial(kernel, n, steps), out_shape=jax.ShapeDt...]
where the time goes in v3:
time: 38.5 us; the launch traced here: 38.2 us
  Pallas kernels  36.2 us (94%)
  local copies, waits for them, and re-layouts  1.35 us (4%)
  between operations  0.64 us (2%)
    pallas_call x1, Pallas kernels, local(): pl.pallas_call(functools.partial(kernel, n, steps), out_shape=jax.ShapeDt...  36.2 us
    slice x1, local copies, waits for them, and re-layouts, local(): return (both[0:1], both[1:2])  1.35 us

profile of v3, /device:TPU:0, one launch (start us, length us, event | category | flops | bytes accessed | tf_op | source)
XLA Modules:
  0.0 38.2 jit_solution(2579769022936783748)
XLA Ops:
  0.6 36.2 %shard_map.50 = f32[2,4,1024]{2,1,0:T(4,128)} custom-call(bf16[1,2,16,16384]{3,2,1,0:T(8,128)(2,1)} %slc_hbm.1, s32[1,4]{1,0:T(1,128)} %flags_hbm.1, bf16[2,2,32]{2,1,0:T(2,128)(2,1)} %taps_hbm.1), custom_call_target="tpu_custom_call" | custom-call | tf_op jit(solution)/shard_map/pallas_call | solution.py:620
  36.9 1.3 %fusion = (f32[1,4,1024]{2,1,0:T(4,128)}, f32[1,4,1024]{2,1,0:T(4,128)}) fusion(f32[2,4,1024]{2,1,0:T(4,128)} %shard_map.50), kind=kLoop, calls=%fused_computation | loop fusion | bytes 65536 | tf_op jit(solution)/shard_map/slice | solution.py:648

commit v4 on v3

--- a/solution.py
+++ b/solution.py
@@ -19,8 +19,9 @@
 SUB = 16
 SIDE = SPAN // 2
 WIN = SPAN + 2 * SIDE
-SLOT = ML_AZ + 1
-LAG = 2
+SLOT = ML_AZ + 2
+REACH = TAPS // 2
+LAG = 3
 
 eps_power = 1e-06
 floor_weight = 0.1
@@ -62,7 +63,7 @@
     n, steps,
     slc_hbm, flags_hbm, taps_hbm, out_ref,
     slc, flags_in, taps_in, taps_ref, turn, data, recv, mat, bands_own, bands_far, both, red, quant,
-    got, pack, back,
+    got, pack, back, place,
     in_sem, send_sem, recv_sem, wave_sem,
 ):
     me = lax.axis_index("date")
@@ -146,7 +147,30 @@
                     data[s, SLOT * (j + 1) + r, :, part * LANES:part * LANES + LANES] = value
         return carry
 
-    lax.fori_loop(0, steps, regroup, 0)
+    tap_lane = lax.broadcasted_iota(jnp.int32, (SUB, LANES), 1)
+
+
+    def edge_at(r, part):
+        return r // 2, (r % 2 * 2 + part) * 2 * REACH
+
+    def send_edges():
+        for s in range(SPAN):
+            packed = [None, None]
+            for r in range(ML_AZ):
+                for part in range(2):
+                    value = data[s, SLOT * steps + r, :, part * LANES:part * LANES + LANES].astype(F32)
+                    tile, at = edge_at(r, part)
+                    head = pltpu.roll(value, at, 1) if at else value
+                    tail = pltpu.roll(value, (at + 2 * REACH) % LANES, 1)
+                    both_ends = jnp.where(tap_lane < at + REACH, head, tail)
+                    old = packed[tile]
+                    packed[tile] = both_ends if old is None else jnp.where(tap_lane >= at, both_ends, old)
+            data[s, SLOT + ML_AZ + 1] = jnp.concatenate(packed, axis=1).astype(BF16)
+
+    regroup(steps - 1, 0)
+    send_edges()
+    regroup(0, 0)
+    regroup(1, 0)
 
     def chunk(ref, j, first):
         return ref.at[pl.ds(SLOT * (j + 1), SLOT if first else ML_AZ)]
@@ -187,10 +211,13 @@
     send_chunk(0, True)
 
     def send_more(j, carry):
+        regroup(j + 1, 0)
         send_chunk(j, False)
         return carry
 
-    lax.fori_loop(1, steps, send_more, 0)
+    lax.fori_loop(1, steps - 2, send_more, 0)
+    for j in range(steps - 2, steps):
+        send_chunk(j, False)
 
     @pl.when(jnp.logical_not(has_left))
     def _():
@@ -201,6 +228,12 @@
     def _():
         for w in range(SIDE + SPAN, WIN):
             recv[w] = jnp.zeros(recv.shape[1:], BF16)
+
+    width = out_ref.shape[2]
+    place_row = lax.broadcasted_iota(jnp.int32, (LANES, width), 0)
+    place_block = lax.broadcasted_iota(jnp.int32, (LANES, width), 1) // CELLS
+    on_place = place_row == lax.rem(place_block, steps) * SUB + place_block // steps
+    place[...] = jnp.where(on_place, 1.0, 0.0).astype(BF16)
 
     sel_row = lax.broadcasted_iota(jnp.int32, (CELLS, 2 * LANES), 0)
     sel_lane = lax.broadcasted_iota(jnp.int32, (CELLS, 2 * LANES), 1)
@@ -238,18 +271,27 @@
             value = jnp.where(sub_row < SUB - 1, pltpu.roll(value, SUB - 1, 1), 0.0)
             recv[w, SLOT * (steps + 1):SLOT * (steps + 1) + ML_AZ] = value.astype(BF16)
 
-    def make_before(dates):
+    def make_edges(dates):
         for w in dates:
-            value = recv[w, SLOT * steps:SLOT * steps + ML_AZ].astype(F32)
-            value = jnp.where(sub_row > 0, pltpu.roll(value, 1, 1), 0.0)
-            recv[w, 0:ML_AZ] = value.astype(BF16)
+            tiles = recv[w, SLOT + ML_AZ + 1].astype(F32)
+            for r in range(ML_AZ):
+                before, after = [], []
+                for part in range(2):
+                    tile, at = edge_at(r, part)
+                    value = tiles[:, tile * LANES:tile * LANES + LANES]
+                    after.append(pltpu.roll(value, LANES - at, 1) if at else value)
+                    value = pltpu.roll(value, (LANES - 2 * REACH - at) % LANES, 1)
+                    before.append(jnp.where(tile_row[:, 0:LANES] > 0, pltpu.roll(value, 1, 0), 0.0))
+                recv[w, r] = jnp.concatenate(before, axis=1).astype(BF16)
+                recv[w, SLOT * (steps + 2) + r] = jnp.concatenate(after, axis=1).astype(BF16)
 
     def band_split(dates, j):
         rows = []
+        behind = SLOT * jnp.where(j == steps - 2, steps + 2, j + 2)
         for w in dates:
             here = recv[w, pl.ds(SLOT * (j + 1), ML_AZ)]
             before = recv[w, pl.ds(SLOT * j, ML_AZ)]
-            after = recv[w, pl.ds(SLOT * (j + 2), ML_AZ)]
+            after = recv[w, pl.ds(behind, ML_AZ)]
             edge = jnp.where(from_before, before, after)
             rows.append(jnp.concatenate([here, edge], axis=2).reshape(ML_AZ * SUB, 4 * LANES))
         made = jnp.dot(jnp.concatenate(rows, axis=0), mat[...], preferred_element_type=F32)
@@ -321,47 +363,47 @@
 
     own_arrive(0, True)
     make_after(OWN)
+    make_edges(OWN)
 
     wave_signal()
 
     def stream(t, carry):
+        u = t - LAG
+
         @pl.when(t < steps)
         def _():
             own_arrive(t, False)
 
-        @pl.when(t == steps - 1)
-        def _():
-            make_before(OWN)
-
         @pl.when(t < slabs)
         def _():
             wave(t, 0)
 
-        @pl.when((t >= 2) & (t < steps + 2))
-        def _():
-            own_step(lax.rem(t - 1, steps))
-
-        @pl.when(t == LAG)
+        @pl.when(t <= steps)
+        def _():
+            own_step(t - 1)
+
+        @pl.when(u == 0)
         def _():
             far_arrive(0, True)
             make_after(FAR)
-
-        @pl.when((t > LAG) & (t < steps + LAG))
-        def _():
-            far_arrive(t - LAG, False)
-
-        @pl.when(t == steps + LAG - 1)
-        def _():
-            make_before(FAR)
-
-        @pl.when(t >= LAG + 2)
-        def _():
-            far_step(lax.rem(t - LAG - 1, steps))
+            make_edges(FAR)
+
+        @pl.when((u > 0) & (u < steps - 1))
+        def _():
+            far_arrive(u, False)
+
+        @pl.when(u > 0)
+        def _():
+            far_step(u - 1)
+
+        @pl.when(u == steps - 1)
+        def _():
+            far_arrive(u, False)
 
         return carry
 
-    lax.fori_loop(1, steps + LAG + 2, stream, 0)
-    lax.fori_loop(steps + LAG + 2, slabs, wave, 0)
+    lax.fori_loop(1, steps + LAG + 1, stream, 0)
+    lax.fori_loop(steps + LAG + 1, slabs, wave, 0)
 
     shape = (steps, CELLS, LANES)
     c_id = lax.broadcasted_iota(jnp.int32, shape, 1)
@@ -584,12 +626,8 @@
     rest = value - high.astype(F32)
     middle = rest.astype(BF16)
     low = (rest - middle.astype(F32)).astype(BF16)
-    width = out_ref.shape[2]
-    place_row = lax.broadcasted_iota(jnp.int32, (LANES, width), 0)
-    place_block = lax.broadcasted_iota(jnp.int32, (LANES, width), 1) // CELLS
-    place = place_row == lax.rem(place_block, steps) * SUB + place_block // steps
     spread = jnp.dot(
-        jnp.concatenate([high, middle, low], axis=0), jnp.where(place, 1.0, 0.0).astype(BF16),
+        jnp.concatenate([high, middle, low], axis=0), place[...],
         preferred_element_type=F32,
     )
     count = 2 * SPAN * CELLS
@@ -612,7 +650,7 @@
     workers = 1
     while 2 * workers <= min(steps, slabs // 2):
         workers *= 2
-    tiles = SLOT * (steps + 2)
+    tiles = SLOT * (steps + 3)
 
     vmem = pl.BlockSpec(memory_space=pltpu.VMEM)
     small = lambda *lead: pltpu.VMEM((*lead, CELLS, LANES), F32)
@@ -639,6 +677,7 @@
             small(slabs, steps // workers, 2 * HALVES),
             small(n),
             small(workers * SPAN),
+            pltpu.VMEM((LANES, span // ML_RG), BF16),
             sem(3), sem(5), sem(3, steps + 2), pltpu.SemaphoreType.REGULAR((2,)),
         ],
         compiler_params=pltpu.CompilerParams(

time: 38.5 us -> 37.5 us (0.974)
  Pallas kernels: 36.2 us -> 35.2 us
    pallas_call x1, Pallas kernels: 36.2 us -> 35.2 us  [local(): pl.pallas_call(functools.partial(kernel, n, steps), out_shape=jax.ShapeDt...]
where the time goes in v4:
time: 37.5 us; the launch traced here: 37.2 us
  Pallas kernels  35.2 us (94%)
  local copies, waits for them, and re-layouts  1.35 us (4%)
  between operations  0.64 us (2%)
    pallas_call x1, Pallas kernels, local(): pl.pallas_call(functools.partial(kernel, n, steps), out_shape=jax.ShapeDt...  35.2 us
    slice x1, local copies, waits for them, and re-layouts, local(): return (both[0:1], both[1:2])  1.35 us

profile of v4, /device:TPU:0, one launch (start us, length us, event | category | flops | bytes accessed | tf_op | source)
XLA Modules:
  0.0 37.2 jit_solution(307389304636280988)
XLA Ops:
  0.6 35.2 %shard_map.50 = f32[2,4,1024]{2,1,0:T(4,128)} custom-call(bf16[1,2,16,16384]{3,2,1,0:T(8,128)(2,1)} %slc_hbm.1, s32[1,4]{1,0:T(1,128)} %flags_hbm.1, bf16[2,2,32]{2,1,0:T(2,128)(2,1)} %taps_hbm.1), custom_call_target="tpu_custom_call" | custom-call | tf_op jit(solution)/shard_map/pallas_call | solution.py:658
  35.9 1.3 %fusion = (f32[1,4,1024]{2,1,0:T(4,128)}, f32[1,4,1024]{2,1,0:T(4,128)}) fusion(f32[2,4,1024]{2,1,0:T(4,128)} %shard_map.50), kind=kLoop, calls=%fused_computation | loop fusion | bytes 65536 | tf_op jit(solution)/shard_map/slice | solution.py:687

commit v5 on v4

--- a/solution.py
+++ b/solution.py
@@ -63,7 +63,7 @@
     n, steps,
     slc_hbm, flags_hbm, taps_hbm, out_ref,
     slc, flags_in, taps_in, taps_ref, turn, data, recv, mat, bands_own, bands_far, both, red, quant,
-    got, pack, back, place,
+    msg, got, pack, back, place,
     in_sem, send_sem, recv_sem, wave_sem,
 ):
     me = lax.axis_index("date")
@@ -455,35 +455,13 @@
         quant[:, h] = den / (2 * RADIUS + 1)
         quant[:, HALVES + h] = num / (den + floor_weight)
 
-    share = got.shape[1]
-    workers = steps // share
+    workers = msg.shape[0]
+    share = steps // workers
     base = (slabs - workers) // 2
     is_worker = (z >= base) & (z < base + workers)
-
-    def line_copy(u):
-        return pltpu.make_async_remote_copy(
-            src_ref=quant.at[pl.ds(u * share, share)], dst_ref=got.at[z],
-            send_sem=send_sem.at[3], recv_sem=recv_sem.at[0, steps],
-            device_id={"date": (base + u) * SPAN + q}, device_id_type=mesh_id,
-        )
-
-    for u in range(workers):
-        @pl.when(z != base + u)
-        def _():
-            line_copy(u).start()
-
-        @pl.when(z == base + u)
-        def _():
-            pltpu.make_async_copy(
-                quant.at[pl.ds(u * share, share)], got.at[z], recv_sem.at[0, steps]
-            ).start()
-
-    def out_copy(target):
-        return pltpu.make_async_remote_copy(
-            src_ref=pack.at[target], dst_ref=back.at[(z - base) * SPAN + q],
-            send_sem=send_sem.at[4], recv_sem=recv_sem.at[0, steps + 1],
-            device_id={"date": target}, device_id_type=mesh_id,
-        )
+    half = LANES // 2
+    ranks = LANES // SUB
+    zero = jnp.zeros((CELLS, LANES), F32)
 
     def turned(rows):
         rows = list(rows)
@@ -498,89 +476,101 @@
             bit *= 2
         return rows
 
-    regs = n * SUB // LANES
-    zero = jnp.zeros((CELLS, LANES), F32)
-    per = LANES // span_lanes
-
-    def gather(jj, kind, k):
-        out = []
-        at = (k - 1) % HALVES * span_lanes
-        for v in range(regs):
-            value = None
-            for m in range(per):
-                piece = got[v * per + m, jj, kind * HALVES + (k - 1) // HALVES]
-                move = (m * span_lanes - at) % LANES
-                piece = pltpu.roll(piece, move, 1) if move else piece
-                value = piece if value is None else jnp.where(lane >= m * span_lanes, piece, value)
-            out.append(value)
-        return out
-
-    def shift(x, dates):
-        far, by = divmod(dates * SUB, LANES)
-        out = []
-        for v in range(regs):
-            low = x[v + far] if 0 <= v + far < regs else zero
-            if by == 0:
-                out.append(low)
-                continue
-            high = x[v + far + 1] if 0 <= v + far + 1 < regs else zero
-            out.append(pltpu.roll(jnp.where(lane >= by, low, high), LANES - by, 1))
-        return out
-
-    def add(x, y):
-        return [a + b for a, b in zip(x, y)]
-
-    def relax(jj):
-        ahead, behind = [], []
-        wsum = [zero] * regs
-        rhs = [zero] * regs
-        for k in range(1, SPAN + 1):
-            skip = SIDE - first_date(k)
-            w = gather(jj, 0, k)
-            p = gather(jj, 1, k)
-            wp = [a * b for a, b in zip(w, p)]
-            ahead.append(shift(w, skip))
-            behind.append(shift(w, skip - k))
-            wsum = add(wsum, add(ahead[-1], behind[-1]))
-            rhs = add(rhs, [b - a for a, b in zip(shift(wp, skip), shift(wp, skip - k))])
-            if k == 1:
-                chain = shift(p, skip)
-        hop = 1
-        while hop < n:
-            chain = add(chain, shift(chain, -hop))
-            hop *= 2
-        chain = shift(chain, -1)
-        rhs = [r + ridge_weight * c for r, c in zip(rhs, chain)]
+    def line_copy(u):
+        return pltpu.make_async_remote_copy(
+            src_ref=msg.at[u], dst_ref=got.at[z],
+            send_sem=send_sem.at[3], recv_sem=recv_sem.at[0, steps],
+            device_id={"date": (base + u) * SPAN + q}, device_id_type=mesh_id,
+        )
+
+    for u in range(workers):
+        for kind in range(2):
+            rows = [zero] * ranks
+            for h in range(HALVES):
+                for jj in range(share):
+                    rows[h * ranks // 2 + jj] = quant[u * share + jj, kind * HALVES + h]
+            for slot, value in enumerate(turned(rows)):
+                msg[u, kind, slot] = value
+
+        @pl.when(z != base + u)
+        def _():
+            line_copy(u).start()
+
+        @pl.when(z == base + u)
+        def _():
+            pltpu.make_async_copy(msg.at[u], got.at[z], recv_sem.at[0, steps]).start()
+
+    def out_copy(target):
+        return pltpu.make_async_remote_copy(
+            src_ref=pack.at[target], dst_ref=back.at[(z - base) * SPAN + q],
+            send_sem=send_sem.at[4], recv_sem=recv_sem.at[0, steps + 1],
+            device_id={"date": target}, device_id_type=mesh_id,
+        )
+
+    in_lower = lane < half
+
+    def split(low, high):
+        return jnp.where(in_lower, low, high)
+
+    def fold(value):
+        return value + pltpu.roll(value, half, 1)
+
+    def at(values, d):
+        return values[d] if 0 <= d < n else zero
+
+    def held(kind, position, d):
+        return got[d // SPAN, kind, position * SPAN + d % SPAN] if d < n else zero
+
+    def relax():
+        near, wide = [], []
+        for kind in range(2):
+            near.append([held(kind, 0, d + 1) for d in range(n)])
+            wide.append([split(held(kind, 1, d + 1), held(kind, 1, d + 2)) for d in range(n)])
+        near_back = [split(at(near[0], d - 1), at(near[0], d - 3)) for d in range(n)]
+        wide_back = [split(at(wide[0], d - 2), at(wide[0], d - 4)) for d in range(n)]
+        wsum = [fold((a + b) + (c + e)) for a, b, c, e in zip(near[0], wide[0], near_back, wide_back)]
+        near_flow = [a * b for a, b in zip(*near)]
+        wide_flow = [a * b for a, b in zip(*wide)]
+        flow = [
+            (split(at(near_flow, d - 1), at(near_flow, d - 3)) + split(at(wide_flow, d - 2), at(wide_flow, d - 4)))
+            - (near_flow[d] + wide_flow[d]) for d in range(n)
+        ]
+        phi = [zero]
+        for d in range(n - 1):
+            first = near[1][d]
+            phi.append(phi[-1] + split(first, pltpu.roll(first, half, 1)))
+        pull = [ridge_weight * p for p in phi]
         inv = [1.0 / (t + ridge_weight) for t in wsum]
-        phi = chain
         for sweep in range(ITERS):
-            acc = rhs
-            for k in range(1, SPAN + 1):
-                acc = add(acc, [a * b for a, b in zip(ahead[k - 1], shift(phi, k))])
-                acc = add(acc, [a * b for a, b in zip(behind[k - 1], shift(phi, -k))])
-            phi = [a * b for a, b in zip(acc, inv)]
+            up = [split(at(phi, d), at(phi, d + 2)) for d in range(n + 2)]
+            down = [split(at(phi, d - 2), at(phi, d - 4)) for d in range(n + 2)]
+            phi = [
+                (
+                    fold(
+                        flow[d] + (near[0][d] * up[d + 1] + wide[0][d] * at(up[:n], d + 2))
+                        + (near_back[d] * down[d + 1] + wide_back[d] * down[d])
+                    ) + pull[d]
+                ) * inv[d] for d in range(n)
+            ]
         return phi, wsum
 
-    half = LANES // 2
-    ranks = LANES // SUB
-
     @pl.when(is_worker)
     def _():
         pltpu.make_async_copy(got, got, recv_sem.at[0, steps]).wait()
-        made = [relax(jj) for jj in range(share)]
-        for v in range(regs):
-            rows = [zero] * ranks
-            for jj in range(share):
-                for kind in range(2):
-                    rows[kind * ranks // 2 + jj] = made[jj][kind][v]
-            for d, value in enumerate(turned(rows)):
-                pack[v * ranks + d] = value
+        phi, wsum = relax()
+        for d in range(n):
+            pack[d] = split(phi[d], wsum[d])
 
         def send_back(i, carry):
-            out_copy(lax.rem(me + i, n)).start()
+            for g in range(SPAN):
+                target = SPAN * jnp.where(z < slabs // 2, slabs - 1 - i, i) + g
+
+                @pl.when(target != me)
+                def _():
+                    out_copy(target).start()
             return carry
 
-        lax.fori_loop(1, n, send_back, 0)
+        lax.fori_loop(0, slabs, send_back, 0)
         pltpu.make_async_copy(
             pack.at[me], back.at[(z - base) * SPAN + q], recv_sem.at[0, steps + 1]
         ).start()
@@ -599,11 +589,11 @@
     def _():
         drain(data.at[pl.ds(0, SIDE), pl.ds(0, tiles)], send_sem.at[2])
 
-    drain(quant.at[pl.ds(0, steps - share)], send_sem.at[3])
+    drain(msg.at[pl.ds(0, workers - 1)], send_sem.at[3])
 
     @pl.when(jnp.logical_not(is_worker))
     def _():
-        drain(quant.at[pl.ds(0, share)], send_sem.at[3])
+        drain(msg.at[0], send_sem.at[3])
 
     drain(back, recv_sem.at[0, steps + 1])
 
@@ -674,7 +664,8 @@
             pltpu.VMEM((steps, SLOTS * SUB, 2 * LANES), BF16),
             pltpu.VMEM((steps, CELLS, SLOTS * SUB), F32),
             small(steps, 2 * HALVES),
-            small(slabs, steps // workers, 2 * HALVES),
+            small(workers, 2, GROUP),
+            small(slabs, 2, GROUP),
             small(n),
             small(workers * SPAN),
             pltpu.VMEM((LANES, span // ML_RG), BF16),

time: 37.5 us -> 36.7 us (0.979)
  Pallas kernels: 35.2 us -> 34.4 us
    pallas_call x1, Pallas kernels: 35.2 us -> 34.4 us  [local(): pl.pallas_call(functools.partial(kernel, n, steps), out_shape=jax.ShapeDt...]
where the time goes in v5:
time: 36.7 us; the launch traced here: 36.4 us
  Pallas kernels  34.4 us (94%)
  local copies, waits for them, and re-layouts  1.35 us (4%)
  between operations  0.64 us (2%)
    pallas_call x1, Pallas kernels, local(): pl.pallas_call(functools.partial(kernel, n, steps), out_shape=jax.ShapeDt...  34.4 us
    slice x1, local copies, waits for them, and re-layouts, local(): return (both[0:1], both[1:2])  1.35 us

profile of v5, /device:TPU:0, one launch (start us, length us, event | category | flops | bytes accessed | tf_op | source)
XLA Modules:
  0.0 36.4 jit_solution(7329950207427672496)
XLA Ops:
  0.6 34.4 %shard_map.50 = f32[2,4,1024]{2,1,0:T(4,128)} custom-call(bf16[1,2,16,16384]{3,2,1,0:T(8,128)(2,1)} %slc_hbm.1, s32[1,4]{1,0:T(1,128)} %flags_hbm.1, bf16[2,2,32]{2,1,0:T(2,128)(2,1)} %taps_hbm.1), custom_call_target="tpu_custom_call" | custom-call | tf_op jit(solution)/shard_map/pallas_call | solution.py:648
  35.1 1.3 %fusion = (f32[1,4,1024]{2,1,0:T(4,128)}, f32[1,4,1024]{2,1,0:T(4,128)}) fusion(f32[2,4,1024]{2,1,0:T(4,128)} %shard_map.50), kind=kLoop, calls=%fused_computation | loop fusion | bytes 65536 | tf_op jit(solution)/shard_map/slice | solution.py:678

commit v6 on v5

--- a/solution.py
+++ b/solution.py
@@ -19,7 +19,7 @@
 SUB = 16
 SIDE = SPAN // 2
 WIN = SPAN + 2 * SIDE
-SLOT = ML_AZ + 2
+SLOT = ML_AZ + 1
 REACH = TAPS // 2
 LAG = 3
 
@@ -63,7 +63,7 @@
     n, steps,
     slc_hbm, flags_hbm, taps_hbm, out_ref,
     slc, flags_in, taps_in, taps_ref, turn, data, recv, mat, bands_own, bands_far, both, red, quant,
-    msg, got, pack, back, place,
+    msg, got, pack, back, place, flag_of,
     in_sem, send_sem, recv_sem, wave_sem,
 ):
     me = lax.axis_index("date")
@@ -98,12 +98,6 @@
     flags_load.wait()
     tile_row = lax.broadcasted_iota(jnp.int32, (SUB, 2 * LANES), 0)
     own_flags = flags_in[...].astype(F32)
-    flag_tile = jnp.zeros((SUB, 2 * LANES), F32)
-    for k in range(SPAN):
-        flag_tile = jnp.where(tile_row == k, jnp.broadcast_to(own_flags[0:1, k:k + 1], flag_tile.shape), flag_tile)
-    flag_tile = flag_tile.astype(BF16)
-    for s in range(SPAN):
-        data[s, SLOT + ML_AZ] = flag_tile
     taps_load.wait()
     taps_ref[...] = jnp.zeros_like(taps_ref)
     for band in range(2):
@@ -163,9 +157,12 @@
                     head = pltpu.roll(value, at, 1) if at else value
                     tail = pltpu.roll(value, (at + 2 * REACH) % LANES, 1)
                     both_ends = jnp.where(tap_lane < at + REACH, head, tail)
+                    if part == 0:
+                        flag = jnp.broadcast_to(own_flags[0:1, r:r + 1], both_ends.shape)
+                        both_ends = jnp.where(tap_lane == at + REACH - 1, flag, both_ends)
                     old = packed[tile]
                     packed[tile] = both_ends if old is None else jnp.where(tap_lane >= at, both_ends, old)
-            data[s, SLOT + ML_AZ + 1] = jnp.concatenate(packed, axis=1).astype(BF16)
+            data[s, SLOT + ML_AZ] = jnp.concatenate(packed, axis=1).astype(BF16)
 
     regroup(steps - 1, 0)
     send_edges()
@@ -273,7 +270,7 @@
 
     def make_edges(dates):
         for w in dates:
-            tiles = recv[w, SLOT + ML_AZ + 1].astype(F32)
+            tiles = recv[w, SLOT + ML_AZ].astype(F32)
             for r in range(ML_AZ):
                 before, after = [], []
                 for part in range(2):
@@ -284,6 +281,19 @@
                     before.append(jnp.where(tile_row[:, 0:LANES] > 0, pltpu.roll(value, 1, 0), 0.0))
                 recv[w, r] = jnp.concatenate(before, axis=1).astype(BF16)
                 recv[w, SLOT * (steps + 2) + r] = jnp.concatenate(after, axis=1).astype(BF16)
+
+    def make_flags():
+        flag_lane = lax.broadcasted_iota(jnp.int32, (CELLS, LANES), 1)
+        for h in range(HALVES):
+            flags = None
+            for slot in range(GROUP):
+                k, g = HALVES * h + slot // SPAN + 1, slot % SPAN
+                tile, at = edge_at(k - 1, 0)
+                at += tile * LANES + REACH - 1
+                tiles = recv[first_date(k) + g, SLOT + ML_AZ].astype(F32)
+                one = jnp.broadcast_to(tiles[0:CELLS, at:at + 1], (CELLS, LANES))
+                flags = one if flags is None else jnp.where(flag_lane >= slot * SUB, one, flags)
+            flag_of[h] = flags
 
     def band_split(dates, j):
         rows = []
@@ -387,6 +397,7 @@
             far_arrive(0, True)
             make_after(FAR)
             make_edges(FAR)
+            make_flags()
 
         @pl.when((u > 0) & (u < steps - 1))
         def _():
@@ -443,12 +454,7 @@
             aligned(power, ks, False) * aligned(power, ks, True) + eps_power
             for power in (register(4 * HALVES), register(4 * HALVES + 1))
         )
-        flag = jnp.zeros((CELLS, LANES), F32)
-        for at, k in enumerate(ks):
-            for g in range(SPAN):
-                one = recv[first_date(k) + g, SLOT + ML_AZ].astype(F32)[k - 1:k, 0:LANES]
-                flag = jnp.where(lane >= (at * SPAN + g) * SUB, jnp.broadcast_to(one, flag.shape), flag)
-        weight = flag[None] * 0.5 * ((cr0 * cr0 + ci0 * ci0) / ab0 + (cr1 * cr1 + ci1 * ci1) / ab1)
+        weight = flag_of[h][None] * 0.5 * ((cr0 * cr0 + ci0 * ci0) / ab0 + (cr1 * cr1 + ci1 * ci1) / ab1)
         phase = split_coef * (ci0 * cr1 - cr0 * ci1) / jnp.sqrt(ab0 * ab1)
         den = box(weight)
         num = box(weight * phase)
@@ -613,15 +619,13 @@
             rows.append(value)
     value = jnp.concatenate(rows, axis=0)
     high = value.astype(BF16)
-    rest = value - high.astype(F32)
-    middle = rest.astype(BF16)
-    low = (rest - middle.astype(F32)).astype(BF16)
+    low = (value - high.astype(F32)).astype(BF16)
     spread = jnp.dot(
-        jnp.concatenate([high, middle, low], axis=0), place[...],
+        jnp.concatenate([high, low], axis=0), place[...],
         preferred_element_type=F32,
     )
     count = 2 * SPAN * CELLS
-    spread = spread[0:count] + spread[count:2 * count] + spread[2 * count:3 * count]
+    spread = spread[0:count] + spread[count:2 * count]
     spread = spread.reshape(2 * SPAN, CELLS, width)
     s_row = lax.broadcasted_iota(jnp.int32, spread.shape, 1)
     s_col = lax.broadcasted_iota(jnp.int32, spread.shape, 2)
@@ -669,6 +673,7 @@
             small(n),
             small(workers * SPAN),
             pltpu.VMEM((LANES, span // ML_RG), BF16),
+            small(HALVES),
             sem(3), sem(5), sem(3, steps + 2), pltpu.SemaphoreType.REGULAR((2,)),
         ],
         compiler_params=pltpu.CompilerParams(

time: 36.7 us -> 36.1 us (0.984)
  Pallas kernels: 34.4 us -> 33.9 us
    pallas_call x1, Pallas kernels: 34.4 us -> 33.9 us  [local(): pl.pallas_call(functools.partial(kernel, n, steps), out_shape=jax.ShapeDt...]
where the time goes in v6:
time: 36.1 us; the launch traced here: 35.9 us
  Pallas kernels  33.9 us (94%)
  local copies, waits for them, and re-layouts  1.35 us (4%)
  between operations  0.64 us (2%)
    pallas_call x1, Pallas kernels, local(): pl.pallas_call(functools.partial(kernel, n, steps), out_shape=jax.ShapeDt...  33.9 us
    slice x1, local copies, waits for them, and re-layouts, local(): return (both[0:1], both[1:2])  1.35 us

profile of v6, /device:TPU:0, one launch (start us, length us, event | category | flops | bytes accessed | tf_op | source)
XLA Modules:
  0.0 35.9 jit_solution(18109180480867968115)
XLA Ops:
  0.6 33.9 %shard_map.50 = f32[2,4,1024]{2,1,0:T(4,128)} custom-call(bf16[1,2,16,16384]{3,2,1,0:T(8,128)(2,1)} %slc_hbm.1, s32[1,4]{1,0:T(1,128)} %flags_hbm.1, bf16[2,2,32]{2,1,0:T(2,128)(2,1)} %taps_hbm.1), custom_call_target="tpu_custom_call" | custom-call | tf_op jit(solution)/shard_map/pallas_call | solution.py:652
  34.5 1.3 %fusion = (f32[1,4,1024]{2,1,0:T(4,128)}, f32[1,4,1024]{2,1,0:T(4,128)}) fusion(f32[2,4,1024]{2,1,0:T(4,128)} %shard_map.50), kind=kLoop, calls=%fused_computation | loop fusion | bytes 65536 | tf_op jit(solution)/shard_map/slice | solution.py:683

commit v7 on v6

--- a/solution.py
+++ b/solution.py
@@ -454,11 +454,13 @@
             aligned(power, ks, False) * aligned(power, ks, True) + eps_power
             for power in (register(4 * HALVES), register(4 * HALVES + 1))
         )
-        weight = flag_of[h][None] * 0.5 * ((cr0 * cr0 + ci0 * ci0) / ab0 + (cr1 * cr1 + ci1 * ci1) / ab1)
-        phase = split_coef * (ci0 * cr1 - cr0 * ci1) / jnp.sqrt(ab0 * ab1)
+        abab = ab0 * ab1
+        shared = (cr0 * cr0 + ci0 * ci0) * ab1 + (cr1 * cr1 + ci1 * ci1) * ab0
+        weight = flag_of[h][None] * 0.5 * (shared / abab)
+        phase = split_coef * (ci0 * cr1 - cr0 * ci1) / jnp.sqrt(abab)
         den = box(weight)
         num = box(weight * phase)
-        quant[:, h] = den / (2 * RADIUS + 1)
+        quant[:, h] = den * (1.0 / (2 * RADIUS + 1))
         quant[:, HALVES + h] = num / (den + floor_weight)
 
     workers = msg.shape[0]

time: 36.1 us -> 36.1 us (level)
  no operation moved by 1% of the time
where the time goes in v7:
time: 36.1 us; the launch traced here: 35.9 us
  Pallas kernels  33.9 us (94%)
  local copies, waits for them, and re-layouts  1.35 us (4%)
  between operations  0.64 us (2%)
    pallas_call x1, Pallas kernels, local(): pl.pallas_call(functools.partial(kernel, n, steps), out_shape=jax.ShapeDt...  33.9 us
    slice x1, local copies, waits for them, and re-layouts, local(): return (both[0:1], both[1:2])  1.35 us

profile of v7, /device:TPU:0, one launch (start us, length us, event | category | flops | bytes accessed | tf_op | source)
XLA Modules:
  0.0 35.9 jit_solution(14910101924425402059)
XLA Ops:
  0.6 33.9 %shard_map.50 = f32[2,4,1024]{2,1,0:T(4,128)} custom-call(bf16[1,2,16,16384]{3,2,1,0:T(8,128)(2,1)} %slc_hbm.1, s32[1,4]{1,0:T(1,128)} %flags_hbm.1, bf16[2,2,32]{2,1,0:T(2,128)(2,1)} %taps_hbm.1), custom_call_target="tpu_custom_call" | custom-call | tf_op jit(solution)/shard_map/pallas_call | solution.py:654
  34.5 1.3 %fusion = (f32[1,4,1024]{2,1,0:T(4,128)}, f32[1,4,1024]{2,1,0:T(4,128)}) fusion(f32[2,4,1024]{2,1,0:T(4,128)} %shard_map.50), kind=kLoop, calls=%fused_computation | loop fusion | bytes 65536 | tf_op jit(solution)/shard_map/slice | solution.py:685

commit v8 on v6

--- a/solution.py
+++ b/solution.py
@@ -413,8 +413,9 @@
 
         return carry
 
-    lax.fori_loop(1, steps + LAG + 1, stream, 0)
-    lax.fori_loop(steps + LAG + 1, slabs, wave, 0)
+    lax.fori_loop(1, steps + LAG, stream, 0)
+    lax.fori_loop(steps + LAG, slabs, wave, 0)
+    far_step(steps - 1)
 
     shape = (steps, CELLS, LANES)
     c_id = lax.broadcasted_iota(jnp.int32, shape, 1)

time: 36.1 us -> 36.2 us (level)
  no operation moved by 1% of the time
where the time goes in v8:
time: 36.2 us; the launch traced here: 36 us
  Pallas kernels  34 us (94%)
  local copies, waits for them, and re-layouts  1.35 us (4%)
  between operations  0.64 us (2%)
    pallas_call x1, Pallas kernels, local(): pl.pallas_call(functools.partial(kernel, n, steps), out_shape=jax.ShapeDt...  34 us
    slice x1, local copies, waits for them, and re-layouts, local(): return (both[0:1], both[1:2])  1.35 us

profile of v8, /device:TPU:0, one launch (start us, length us, event | category | flops | bytes accessed | tf_op | source)
XLA Modules:
  0.0 36.0 jit_solution(8916762963172233892)
XLA Ops:
  0.6 34.0 %shard_map.50 = f32[2,4,1024]{2,1,0:T(4,128)} custom-call(bf16[1,2,16,16384]{3,2,1,0:T(8,128)(2,1)} %slc_hbm.1, s32[1,4]{1,0:T(1,128)} %flags_hbm.1, bf16[2,2,32]{2,1,0:T(2,128)(2,1)} %taps_hbm.1), custom_call_target="tpu_custom_call" | custom-call | tf_op jit(solution)/shard_map/pallas_call | solution.py:653
  34.6 1.3 %fusion = (f32[1,4,1024]{2,1,0:T(4,128)}, f32[1,4,1024]{2,1,0:T(4,128)}) fusion(f32[2,4,1024]{2,1,0:T(4,128)} %shard_map.50), kind=kLoop, calls=%fused_computation | loop fusion | bytes 65536 | tf_op jit(solution)/shard_map/slice | solution.py:684
